TPU v7x, 32 devices: a whole 2x2x4 slice. The times are simulated.
32 devices in a mesh: groups: 2 (over y), shot: 8 (over z, x), slab: 2 (over core).
Axes of the slice: x: 2, y: 2, z: 4, core: 2. Of those that a mesh axis runs over, the one named last changes fastest.
Arguments:
- field_now: float32 [64, 8192], P('slab', ('groups', 'shot')), parts along dimension 1, may hold values from -6 to 6
- field_before: float32 [64, 8192], P('slab', ('groups', 'shot')), parts along dimension 1, may hold values from -6 to 6
- velocity: bfloat16 [64, 2048], P('slab', ('groups', 'shot')), parts along dimension 1, may hold values from 5 to 5.4375
- offsets: int32 [16], P(('groups', 'shot')), parts along dimension 0, may hold values from 0 to 512
- source_cell: int32 [16], P(('groups', 'shot')), parts along dimension 0, may hold values from 0 to 32767
- traces: bfloat16 [2, 4096, 256], P('slab', ('groups', 'shot')), parts along dimension 1, may hold values from -6 to 6
- trace_shot: int32 [2, 4096, 1], P('slab', ('groups', 'shot')), parts along dimension 1, may hold values from 0 to 7; in each aligned block of 256 rows (0 to 255, 256 to 511, ..., all dimensions but the last counted through in order) at most 64 rows name the same one
- trace_node_cell: int32 [2, 4096], P('slab', ('groups', 'shot')), parts along dimension 1, may hold values from 0 to 16383
Outputs:
- pressure: float32 [64, 8192], P('slab', ('groups', 'shot')), parts along dimension 1
There are 2 independent parts, one for each index of `groups`. A program takes and returns all parts, laid end to end along the dimension named above; each array names one. Nothing has to cross between parts.
Inputs may be any that keep to these rules, and one draw needn't show every extreme that they name: `trace_shot`: among the trace rows of one device (aligned blocks of 256 rows along the second dimension, for each slab) at most 64 belong to one shot, and in some block some shot has exactly 64.
All inputs are finite; a program needn't handle non-finite values.
Results may differ from a plain program's by a relative error of at most 0.0003.
Values may be sent and summed in bfloat16 or wider, within the bound.
A program may use at most 64 MiB of HBM per device.

v0:
```python
import math

import jax
import jax.numpy as jnp
from jax import lax
from jax.sharding import PartitionSpec as P

NS = 256
STEPS = 24
CAP = 64


LAP_CENTER = -205.0 / 72.0
LAP_TAPS = (1.6, -0.2, 8.0 / 315.0, -1.0 / 560.0)
PEAK = 0.12
DELAY = 5.0
SOURCE_GAIN = 2.0
RATIO = 0.1


def extended(cells, sides, width):
    for axis, dim in sides:
        count = lax.axis_size(axis)
        ends = count - 1
        head = lax.slice_in_dim(cells, 0, width, axis=dim)
        tail = lax.slice_in_dim(cells, cells.shape[dim] - width, cells.shape[dim], axis=dim)
        cells = jnp.concatenate(
            [
                lax.ppermute(tail, axis, [(i, (i + 1) % count) for i in range(ends)]),
                cells,
                lax.ppermute(head, axis, [((i + 1) % count, i) for i in range(ends)]),
            ],
            axis=dim,
        )
    return cells


def sample_table(sample_values, steps):
    kernel_step_index = jnp.arange(sample_values, dtype=jnp.float32)[:, None] + 0.5
    time_index = jnp.arange(steps, dtype=jnp.float32)[None, :] + 1.0
    return jnp.cos(math.pi * kernel_step_index * time_index / sample_values) * math.sqrt(
        2.0 / sample_values
    )


def ricker(step_value):
    argument = (math.pi * PEAK * (step_value - DELAY)) ** 2
    return (1.0 - 2.0 * argument) * jnp.exp(-argument)


def laplace(depth_padded, wavefield):
    depth_rows = wavefield.shape[-2]
    width_cols = wavefield.shape[-1]
    pads = [(0, 0)] * (wavefield.ndim - 1) + [(4, 4)]
    lateral_pad = jnp.pad(wavefield, pads)
    running_total = 2.0 * LAP_CENTER * wavefield
    for distance in range(1, 5):
        coeff = LAP_TAPS[distance - 1]
        running_total = running_total + coeff * (
            depth_padded[..., 4 + distance : 4 + distance + depth_rows, :]
            + depth_padded[..., 4 - distance : 4 - distance + depth_rows, :]
        )
        running_total = running_total + coeff * (
            lateral_pad[..., 4 + distance : 4 + distance + width_cols]
            + lateral_pad[..., 4 - distance : 4 - distance + width_cols]
        )
    return running_total


def local(
    field_now, field_before, velocity, offsets, source_cell, traces, trace_shot, trace_node_cell
):
    depth_rows, width_cols = field_now.shape
    shots = lax.axis_size("shot")
    anchor_point = offsets[0]
    panel_part = lax.all_gather(velocity, "shot", axis=1, tiled=True)
    span = panel_part.shape[1]
    column_index = anchor_point + jnp.arange(width_cols, dtype=jnp.int32)
    inside = (column_index >= 0) & (column_index < span)
    picked = jnp.take(panel_part, jnp.clip(column_index, 0, span - 1), axis=1)
    window = jnp.where(inside[None, :], picked.astype(jnp.float32), 0.0)
    courant = jnp.square(window * RATIO)
    target = trace_shot[0, :, 0]
    onehot = (target[:, None] == jnp.arange(shots, dtype=jnp.int32)[None, :]).astype(jnp.int32)
    position = jnp.sum(jnp.cumsum(onehot, axis=0) * onehot, axis=1) - 1
    slot_position_index = target * CAP + position
    table = sample_table(NS, STEPS)
    node_buffer = (
        jnp.zeros((shots * CAP,), jnp.int32)
        .at[slot_position_index]
        .set(trace_node_cell[0])
        .reshape(shots, CAP)
    )
    trace_buffer = (
        jnp.zeros((shots * CAP, NS), jnp.bfloat16)
        .at[slot_position_index]
        .set(traces[0])
        .reshape(shots, CAP, NS)
    )
    trace_rows = lax.all_to_all(trace_buffer, "shot", split_axis=0, concat_axis=0, tiled=True)
    node_rows = lax.all_to_all(node_buffer, "shot", split_axis=0, concat_axis=0, tiled=True)
    stepped = jnp.einsum(
        "sck,kt->sct", trace_rows.astype(jnp.float32), table, precision=lax.Precision.HIGHEST
    )
    amplitude, node_rows = (stepped, node_rows)
    amplitude = amplitude.reshape(-1, STEPS)
    node_rows = node_rows.reshape(-1)
    injections = (
        jnp.zeros((STEPS, depth_rows * width_cols), jnp.float32).at[:, node_rows].add(amplitude.T)
    )
    injections = injections.reshape(STEPS, depth_rows, width_cols)
    source_index = source_cell[0]
    local_depth = source_index // width_cols - lax.axis_index("slab") * depth_rows
    lateral = source_index % width_cols
    source_mask = (
        (jnp.arange(depth_rows, dtype=jnp.int32)[:, None] == local_depth)
        & (jnp.arange(width_cols, dtype=jnp.int32)[None, :] == lateral)
    ).astype(jnp.float32)

    def inject(step):
        injection = lax.dynamic_index_in_dim(injections, step, 0, keepdims=False)
        return injection + SOURCE_GAIN * ricker(step.astype(jnp.float32)) * source_mask

    def advance(step, carry):
        present, earlier = carry
        injection = inject(step)
        depth_padded = extended(present, (("slab", 0),), 4)
        advanced = 2.0 * present - earlier + courant * laplace(depth_padded, present) + injection
        return (advanced, present)

    present, earlier = lax.fori_loop(0, STEPS, advance, (field_now, field_before))
    return present


def solution(mesh):
    in_specs = (
        P("slab", ("groups", "shot")),
        P("slab", ("groups", "shot")),
        P("slab", ("groups", "shot")),
        P(("groups", "shot")),
        P(("groups", "shot")),
        P("slab", ("groups", "shot"), None),
        P("slab", ("groups", "shot"), None),
        P("slab", ("groups", "shot")),
    )
    out_specs = P("slab", ("groups", "shot"))
    return jax.shard_map(local, mesh=mesh, in_specs=in_specs, out_specs=out_specs, check_vma=False)
```

profile of v0, /device:TPU:0, one launch (start us, length us, event | category | flops | bytes accessed | tf_op | source)
XLA Modules:
  0.0 207.0 jit_solution(2775236064112403542)
XLA Ops:
  5.2 7.3 %all-to-all-start = ((s32[8,1,64]{2,1,0:T(1,128)}), s32[8,1,64]{2,1,0:T(1,128)S(1)}, u32[]{:S(2)}, u32[]{:S(2)}) async-start(s32[8,1,64]{2,1,0:T(1,128)} %all_to_all.9), calls=%async_computation | async-start | bytes 8192 | tf_op jit(solution)/shard_map/all_to_all | solution.py:101
  14.0 31.3 %all_gather.3 = bf16[32,1024]{0,1:T(8,128)(2,1)S(1)} all-gather(bf16[32,128]{0,1:T(8,128)(2,1)S(1)} %copy.17), channel_id=1, replica_groups=mesh['groups'=2,'shot'=8,'slab'=2] {'shot'}, dimensions={1}, use_global_device_ids=true | all-gather | bytes 73728 | tf_op jit(solution)/shard_map/all_gather | solution.py:76
  47.5 2.1 %scatter_custom_fusion.1 = bf16[512,256]{1,0:T(8,128)(2,1)} fusion(s32[256]{0:T(256)S(1)} %bitcast.49, bf16[1,256,256]{2,1,0:T(8,128)(2,1)S(1)} %copy-done, bf16[]{:T(256)} %constant.223.clone.1), kind=kCustom, calls=%fused_computation.56 | custom fusion | bytes 393218 | tf_op jit(solution)/shard_map/scatter | solution.py:97
  49.7 5.4 %all-to-all-start.1 = ((bf16[8,64,256]{2,1,0:T(8,128)(2,1)}), bf16[8,64,256]{2,1,0:T(8,128)(2,1)S(1)}, u32[]{:S(2)}, u32[]{:S(2)}) async-start(bf16[8,64,256]{2,1,0:T(8,128)(2,1)} %bitcast.13), calls=%async_computation.1 | async-start | bytes 524288 | tf_op jit(solution)/shard_map/all_to_all | solution.py:100
  56.6 6.8 %all-to-all-done.1 = bf16[8,64,256]{2,1,0:T(8,128)(2,1)S(1)} async-done(((bf16[8,64,256]{2,1,0:T(8,128)(2,1)}), bf16[8,64,256]{2,1,0:T(8,128)(2,1)S(1)}, u32[]{:S(2)}, u32[]{:S(2)}) %all-to-all-start.1) | async-done | bytes 262176 | tf_op jit(solution)/shard_map/all_to_all | solution.py:100
  63.9 7.1 %scatter_custom_fusion.2 = f32[24,16384]{0,1:T(8,128)} fusion(s32[512]{0:T(512)S(1)} %bitcast.47, f32[512,24]{1,0:T(8,128)S(1)} %bitcast.42, f32[]{:T(128)} %constant.218.clone.1), kind=kCustom, calls=%fused_computation.53 | custom fusion | flops 12288 | bytes 1572868 | tf_op jit(solution)/shard_map/scatter-add | solution.py:109
  71.0 5.3 %copy.21 = f32[24,32,512]{2,1,0:T(8,128)S(1)} copy(f32[24,32,512]{0,2,1:T(8,128)} %bitcast.41) | data formatting | bytes 3145728
  76.3 130.0 %while.20 = (s32[]{:T(128)}, f32[32,512]{1,0:T(8,128)S(1)}, f32[32,512]{1,0:T(8,128)S(1)}, f32[32,512]{1,0:T(8,128)S(1)}, f32[24,32,512]{2,1,0:T(8,128)S(1)}, /*...) while((s32[]{:T(128)}, f32[32,512]{1,0:T(8,128)S(1)}, ...), condition=%wide.region_7.8_spmd.clone, body=%wide.region_6.7_spmd.clone.sunk | while | flops 606219 | bytes 1106793 | solution.py:131
  77.7 3.0 %collective-permute-start = (f32[4,512]{1,0:T(4,128)S(1)}, f32[4,512]{1,0:T(4,128)S(1)}, u32[]{:S(2)}, u32[]{:S(2)}) collective-permute-start(f32[4,512]{1,0:T(4,128)S(1)} %get-tuple-element.309), channel_id=1, source_target_pairs={{0,1},{2,3},{4,5},{6,7},{8,9},{10,11},{12,13},{14,15},{16,17},{18,... | collective-permute-start | bytes 24584 | tf_op jit(solution)/shard_map/while/body/eval_jaxpr/ppermute | solution.py:29
  83.1 3.0 %collective-permute-start = (f32[4,512]{1,0:T(4,128)S(1)}, f32[4,512]{1,0:T(4,128)S(1)}, u32[]{:S(2)}, u32[]{:S(2)}) collective-permute-start(f32[4,512]{1,0:T(4,128)S(1)} %get-tuple-element.309), channel_id=1, source_target_pairs={{0,1},{2,3},{4,5},{6,7},{8,9},{10,11},{12,13},{14,15},{16,17},{18,... | collective-permute-start | bytes 24584 | tf_op jit(solution)/shard_map/while/body/eval_jaxpr/ppermute | solution.py:29
  88.5 3.0 %collective-permute-start = (f32[4,512]{1,0:T(4,128)S(1)}, f32[4,512]{1,0:T(4,128)S(1)}, u32[]{:S(2)}, u32[]{:S(2)}) collective-permute-start(f32[4,512]{1,0:T(4,128)S(1)} %get-tuple-element.309), channel_id=1, source_target_pairs={{0,1},{2,3},{4,5},{6,7},{8,9},{10,11},{12,13},{14,15},{16,17},{18,... | collective-permute-start | bytes 24584 | tf_op jit(solution)/shard_map/while/body/eval_jaxpr/ppermute | solution.py:29
  93.9 3.0 %collective-permute-start = (f32[4,512]{1,0:T(4,128)S(1)}, f32[4,512]{1,0:T(4,128)S(1)}, u32[]{:S(2)}, u32[]{:S(2)}) collective-permute-start(f32[4,512]{1,0:T(4,128)S(1)} %get-tuple-element.309), channel_id=1, source_target_pairs={{0,1},{2,3},{4,5},{6,7},{8,9},{10,11},{12,13},{14,15},{16,17},{18,... | collective-permute-start | bytes 24584 | tf_op jit(solution)/shard_map/while/body/eval_jaxpr/ppermute | solution.py:29
  99.3 3.0 %collective-permute-start = (f32[4,512]{1,0:T(4,128)S(1)}, f32[4,512]{1,0:T(4,128)S(1)}, u32[]{:S(2)}, u32[]{:S(2)}) collective-permute-start(f32[4,512]{1,0:T(4,128)S(1)} %get-tuple-element.309), channel_id=1, source_target_pairs={{0,1},{2,3},{4,5},{6,7},{8,9},{10,11},{12,13},{14,15},{16,17},{18,... | collective-permute-start | bytes 24584 | tf_op jit(solution)/shard_map/while/body/eval_jaxpr/ppermute | solution.py:29
  104.7 3.0 %collective-permute-start = (f32[4,512]{1,0:T(4,128)S(1)}, f32[4,512]{1,0:T(4,128)S(1)}, u32[]{:S(2)}, u32[]{:S(2)}) collective-permute-start(f32[4,512]{1,0:T(4,128)S(1)} %get-tuple-element.309), channel_id=1, source_target_pairs={{0,1},{2,3},{4,5},{6,7},{8,9},{10,11},{12,13},{14,15},{16,17},{18,... | collective-permute-start | bytes 24584 | tf_op jit(solution)/shard_map/while/body/eval_jaxpr/ppermute | solution.py:29
  110.2 3.0 %collective-permute-start = (f32[4,512]{1,0:T(4,128)S(1)}, f32[4,512]{1,0:T(4,128)S(1)}, u32[]{:S(2)}, u32[]{:S(2)}) collective-permute-start(f32[4,512]{1,0:T(4,128)S(1)} %get-tuple-element.309), channel_id=1, source_target_pairs={{0,1},{2,3},{4,5},{6,7},{8,9},{10,11},{12,13},{14,15},{16,17},{18,... | collective-permute-start | bytes 24584 | tf_op jit(solution)/shard_map/while/body/eval_jaxpr/ppermute | solution.py:29
  115.6 3.0 %collective-permute-start = (f32[4,512]{1,0:T(4,128)S(1)}, f32[4,512]{1,0:T(4,128)S(1)}, u32[]{:S(2)}, u32[]{:S(2)}) collective-permute-start(f32[4,512]{1,0:T(4,128)S(1)} %get-tuple-element.309), channel_id=1, source_target_pairs={{0,1},{2,3},{4,5},{6,7},{8,9},{10,11},{12,13},{14,15},{16,17},{18,... | collective-permute-start | bytes 24584 | tf_op jit(solution)/shard_map/while/body/eval_jaxpr/ppermute | solution.py:29
  121.0 3.0 %collective-permute-start = (f32[4,512]{1,0:T(4,128)S(1)}, f32[4,512]{1,0:T(4,128)S(1)}, u32[]{:S(2)}, u32[]{:S(2)}) collective-permute-start(f32[4,512]{1,0:T(4,128)S(1)} %get-tuple-element.309), channel_id=1, source_target_pairs={{0,1},{2,3},{4,5},{6,7},{8,9},{10,11},{12,13},{14,15},{16,17},{18,... | collective-permute-start | bytes 24584 | tf_op jit(solution)/shard_map/while/body/eval_jaxpr/ppermute | solution.py:29
  126.4 3.0 %collective-permute-start = (f32[4,512]{1,0:T(4,128)S(1)}, f32[4,512]{1,0:T(4,128)S(1)}, u32[]{:S(2)}, u32[]{:S(2)}) collective-permute-start(f32[4,512]{1,0:T(4,128)S(1)} %get-tuple-element.309), channel_id=1, source_target_pairs={{0,1},{2,3},{4,5},{6,7},{8,9},{10,11},{12,13},{14,15},{16,17},{18,... | collective-permute-start | bytes 24584 | tf_op jit(solution)/shard_map/while/body/eval_jaxpr/ppermute | solution.py:29
  131.8 3.0 %collective-permute-start = (f32[4,512]{1,0:T(4,128)S(1)}, f32[4,512]{1,0:T(4,128)S(1)}, u32[]{:S(2)}, u32[]{:S(2)}) collective-permute-start(f32[4,512]{1,0:T(4,128)S(1)} %get-tuple-element.309), channel_id=1, source_target_pairs={{0,1},{2,3},{4,5},{6,7},{8,9},{10,11},{12,13},{14,15},{16,17},{18,... | collective-permute-start | bytes 24584 | tf_op jit(solution)/shard_map/while/body/eval_jaxpr/ppermute | solution.py:29
  137.2 3.0 %collective-permute-start = (f32[4,512]{1,0:T(4,128)S(1)}, f32[4,512]{1,0:T(4,128)S(1)}, u32[]{:S(2)}, u32[]{:S(2)}) collective-permute-start(f32[4,512]{1,0:T(4,128)S(1)} %get-tuple-element.309), channel_id=1, source_target_pairs={{0,1},{2,3},{4,5},{6,7},{8,9},{10,11},{12,13},{14,15},{16,17},{18,... | collective-permute-start | bytes 24584 | tf_op jit(solution)/shard_map/while/body/eval_jaxpr/ppermute | solution.py:29
  142.7 3.0 %collective-permute-start = (f32[4,512]{1,0:T(4,128)S(1)}, f32[4,512]{1,0:T(4,128)S(1)}, u32[]{:S(2)}, u32[]{:S(2)}) collective-permute-start(f32[4,512]{1,0:T(4,128)S(1)} %get-tuple-element.309), channel_id=1, source_target_pairs={{0,1},{2,3},{4,5},{6,7},{8,9},{10,11},{12,13},{14,15},{16,17},{18,... | collective-permute-start | bytes 24584 | tf_op jit(solution)/shard_map/while/body/eval_jaxpr/ppermute | solution.py:29
  148.1 3.0 %collective-permute-start = (f32[4,512]{1,0:T(4,128)S(1)}, f32[4,512]{1,0:T(4,128)S(1)}, u32[]{:S(2)}, u32[]{:S(2)}) collective-permute-start(f32[4,512]{1,0:T(4,128)S(1)} %get-tuple-element.309), channel_id=1, source_target_pairs={{0,1},{2,3},{4,5},{6,7},{8,9},{10,11},{12,13},{14,15},{16,17},{18,... | collective-permute-start | bytes 24584 | tf_op jit(solution)/shard_map/while/body/eval_jaxpr/ppermute | solution.py:29
  153.5 3.0 %collective-permute-start = (f32[4,512]{1,0:T(4,128)S(1)}, f32[4,512]{1,0:T(4,128)S(1)}, u32[]{:S(2)}, u32[]{:S(2)}) collective-permute-start(f32[4,512]{1,0:T(4,128)S(1)} %get-tuple-element.309), channel_id=1, source_target_pairs={{0,1},{2,3},{4,5},{6,7},{8,9},{10,11},{12,13},{14,15},{16,17},{18,... | collective-permute-start | bytes 24584 | tf_op jit(solution)/shard_map/while/body/eval_jaxpr/ppermute | solution.py:29
  158.9 3.0 %collective-permute-start = (f32[4,512]{1,0:T(4,128)S(1)}, f32[4,512]{1,0:T(4,128)S(1)}, u32[]{:S(2)}, u32[]{:S(2)}) collective-permute-start(f32[4,512]{1,0:T(4,128)S(1)} %get-tuple-element.309), channel_id=1, source_target_pairs={{0,1},{2,3},{4,5},{6,7},{8,9},{10,11},{12,13},{14,15},{16,17},{18,... | collective-permute-start | bytes 24584 | tf_op jit(solution)/shard_map/while/body/eval_jaxpr/ppermute | solution.py:29
  164.3 3.0 %collective-permute-start = (f32[4,512]{1,0:T(4,128)S(1)}, f32[4,512]{1,0:T(4,128)S(1)}, u32[]{:S(2)}, u32[]{:S(2)}) collective-permute-start(f32[4,512]{1,0:T(4,128)S(1)} %get-tuple-element.309), channel_id=1, source_target_pairs={{0,1},{2,3},{4,5},{6,7},{8,9},{10,11},{12,13},{14,15},{16,17},{18,... | collective-permute-start | bytes 24584 | tf_op jit(solution)/shard_map/while/body/eval_jaxpr/ppermute | solution.py:29
  169.7 3.0 %collective-permute-start = (f32[4,512]{1,0:T(4,128)S(1)}, f32[4,512]{1,0:T(4,128)S(1)}, u32[]{:S(2)}, u32[]{:S(2)}) collective-permute-start(f32[4,512]{1,0:T(4,128)S(1)} %get-tuple-element.309), channel_id=1, source_target_pairs={{0,1},{2,3},{4,5},{6,7},{8,9},{10,11},{12,13},{14,15},{16,17},{18,... | collective-permute-start | bytes 24584 | tf_op jit(solution)/shard_map/while/body/eval_jaxpr/ppermute | solution.py:29
  175.2 3.0 %collective-permute-start = (f32[4,512]{1,0:T(4,128)S(1)}, f32[4,512]{1,0:T(4,128)S(1)}, u32[]{:S(2)}, u32[]{:S(2)}) collective-permute-start(f32[4,512]{1,0:T(4,128)S(1)} %get-tuple-element.309), channel_id=1, source_target_pairs={{0,1},{2,3},{4,5},{6,7},{8,9},{10,11},{12,13},{14,15},{16,17},{18,... | collective-permute-start | bytes 24584 | tf_op jit(solution)/shard_map/while/body/eval_jaxpr/ppermute | solution.py:29
  180.6 3.0 %collective-permute-start = (f32[4,512]{1,0:T(4,128)S(1)}, f32[4,512]{1,0:T(4,128)S(1)}, u32[]{:S(2)}, u32[]{:S(2)}) collective-permute-start(f32[4,512]{1,0:T(4,128)S(1)} %get-tuple-element.309), channel_id=1, source_target_pairs={{0,1},{2,3},{4,5},{6,7},{8,9},{10,11},{12,13},{14,15},{16,17},{18,... | collective-permute-start | bytes 24584 | tf_op jit(solution)/shard_map/while/body/eval_jaxpr/ppermute | solution.py:29
  186.0 3.0 %collective-permute-start = (f32[4,512]{1,0:T(4,128)S(1)}, f32[4,512]{1,0:T(4,128)S(1)}, u32[]{:S(2)}, u32[]{:S(2)}) collective-permute-start(f32[4,512]{1,0:T(4,128)S(1)} %get-tuple-element.309), channel_id=1, source_target_pairs={{0,1},{2,3},{4,5},{6,7},{8,9},{10,11},{12,13},{14,15},{16,17},{18,... | collective-permute-start | bytes 24584 | tf_op jit(solution)/shard_map/while/body/eval_jaxpr/ppermute | solution.py:29
  191.4 3.0 %collective-permute-start = (f32[4,512]{1,0:T(4,128)S(1)}, f32[4,512]{1,0:T(4,128)S(1)}, u32[]{:S(2)}, u32[]{:S(2)}) collective-permute-start(f32[4,512]{1,0:T(4,128)S(1)} %get-tuple-element.309), channel_id=1, source_target_pairs={{0,1},{2,3},{4,5},{6,7},{8,9},{10,11},{12,13},{14,15},{16,17},{18,... | collective-permute-start | bytes 24584 | tf_op jit(solution)/shard_map/while/body/eval_jaxpr/ppermute | solution.py:29
  196.8 3.0 %collective-permute-start = (f32[4,512]{1,0:T(4,128)S(1)}, f32[4,512]{1,0:T(4,128)S(1)}, u32[]{:S(2)}, u32[]{:S(2)}) collective-permute-start(f32[4,512]{1,0:T(4,128)S(1)} %get-tuple-element.309), channel_id=1, source_target_pairs={{0,1},{2,3},{4,5},{6,7},{8,9},{10,11},{12,13},{14,15},{16,17},{18,... | collective-permute-start | bytes 24584 | tf_op jit(solution)/shard_map/while/body/eval_jaxpr/ppermute | solution.py:29
  202.2 3.0 %collective-permute-start = (f32[4,512]{1,0:T(4,128)S(1)}, f32[4,512]{1,0:T(4,128)S(1)}, u32[]{:S(2)}, u32[]{:S(2)}) collective-permute-start(f32[4,512]{1,0:T(4,128)S(1)} %get-tuple-element.309), channel_id=1, source_target_pairs={{0,1},{2,3},{4,5},{6,7},{8,9},{10,11},{12,13},{14,15},{16,17},{18,... | collective-permute-start | bytes 24584 | tf_op jit(solution)/shard_map/while/body/eval_jaxpr/ppermute | solution.py:29
  (251 shorter events, 64.4 us)
Async XLA Ops:
  5.2 44.4 %all-to-all-start = ((s32[8,1,64]{2,1,0:T(1,128)}), s32[8,1,64]{2,1,0:T(1,128)S(1)}, u32[]{:S(2)}, u32[]{:S(2)}) async-start(s32[8,1,64]{2,1,0:T(1,128)} %all_to_all.9), calls=%async_computation | async-start | bytes 8192 | tf_op jit(solution)/shard_map/all_to_all | solution.py:101
  49.7 13.7 %all-to-all-start.1 = ((bf16[8,64,256]{2,1,0:T(8,128)(2,1)}), bf16[8,64,256]{2,1,0:T(8,128)(2,1)S(1)}, u32[]{:S(2)}, u32[]{:S(2)}) async-start(bf16[8,64,256]{2,1,0:T(8,128)(2,1)} %bitcast.13), calls=%async_computation.1 | async-start | bytes 524288 | tf_op jit(solution)/shard_map/all_to_all | solution.py:100
  76.4 4.4 %collective-permute-start.1 = (f32[4,512]{1,0:T(4,128)S(1)}, f32[4,512]{1,0:T(4,128)S(1)}, u32[]{:S(2)}, u32[]{:S(2)}) collective-permute-start(f32[4,512]{1,0:T(4,128)S(1)} %get-tuple-element.310), channel_id=1, source_target_pairs={{1,0},{3,2},{5,4},{7,6},{9,8},{11,10},{13,12},{15,14},{17,16},{19,... | collective-permute-start | bytes 24584 | tf_op jit(solution)/shard_map/while/body/eval_jaxpr/ppermute | solution.py:31
  81.8 4.4 %collective-permute-start.1 = (f32[4,512]{1,0:T(4,128)S(1)}, f32[4,512]{1,0:T(4,128)S(1)}, u32[]{:S(2)}, u32[]{:S(2)}) collective-permute-start(f32[4,512]{1,0:T(4,128)S(1)} %get-tuple-element.310), channel_id=1, source_target_pairs={{1,0},{3,2},{5,4},{7,6},{9,8},{11,10},{13,12},{15,14},{17,16},{19,... | collective-permute-start | bytes 24584 | tf_op jit(solution)/shard_map/while/body/eval_jaxpr/ppermute | solution.py:31
  83.1 3.8 %collective-permute-start = (f32[4,512]{1,0:T(4,128)S(1)}, f32[4,512]{1,0:T(4,128)S(1)}, u32[]{:S(2)}, u32[]{:S(2)}) collective-permute-start(f32[4,512]{1,0:T(4,128)S(1)} %get-tuple-element.309), channel_id=1, source_target_pairs={{0,1},{2,3},{4,5},{6,7},{8,9},{10,11},{12,13},{14,15},{16,17},{18,... | collective-permute-start | bytes 24584 | tf_op jit(solution)/shard_map/while/body/eval_jaxpr/ppermute | solution.py:29
  87.2 4.4 %collective-permute-start.1 = (f32[4,512]{1,0:T(4,128)S(1)}, f32[4,512]{1,0:T(4,128)S(1)}, u32[]{:S(2)}, u32[]{:S(2)}) collective-permute-start(f32[4,512]{1,0:T(4,128)S(1)} %get-tuple-element.310), channel_id=1, source_target_pairs={{1,0},{3,2},{5,4},{7,6},{9,8},{11,10},{13,12},{15,14},{17,16},{19,... | collective-permute-start | bytes 24584 | tf_op jit(solution)/shard_map/while/body/eval_jaxpr/ppermute | solution.py:31
  88.5 3.8 %collective-permute-start = (f32[4,512]{1,0:T(4,128)S(1)}, f32[4,512]{1,0:T(4,128)S(1)}, u32[]{:S(2)}, u32[]{:S(2)}) collective-permute-start(f32[4,512]{1,0:T(4,128)S(1)} %get-tuple-element.309), channel_id=1, source_target_pairs={{0,1},{2,3},{4,5},{6,7},{8,9},{10,11},{12,13},{14,15},{16,17},{18,... | collective-permute-start | bytes 24584 | tf_op jit(solution)/shard_map/while/body/eval_jaxpr/ppermute | solution.py:29
  92.6 4.4 %collective-permute-start.1 = (f32[4,512]{1,0:T(4,128)S(1)}, f32[4,512]{1,0:T(4,128)S(1)}, u32[]{:S(2)}, u32[]{:S(2)}) collective-permute-start(f32[4,512]{1,0:T(4,128)S(1)} %get-tuple-element.310), channel_id=1, source_target_pairs={{1,0},{3,2},{5,4},{7,6},{9,8},{11,10},{13,12},{15,14},{17,16},{19,... | collective-permute-start | bytes 24584 | tf_op jit(solution)/shard_map/while/body/eval_jaxpr/ppermute | solution.py:31
  93.9 3.8 %collective-permute-start = (f32[4,512]{1,0:T(4,128)S(1)}, f32[4,512]{1,0:T(4,128)S(1)}, u32[]{:S(2)}, u32[]{:S(2)}) collective-permute-start(f32[4,512]{1,0:T(4,128)S(1)} %get-tuple-element.309), channel_id=1, source_target_pairs={{0,1},{2,3},{4,5},{6,7},{8,9},{10,11},{12,13},{14,15},{16,17},{18,... | collective-permute-start | bytes 24584 | tf_op jit(solution)/shard_map/while/body/eval_jaxpr/ppermute | solution.py:29
  98.0 4.4 %collective-permute-start.1 = (f32[4,512]{1,0:T(4,128)S(1)}, f32[4,512]{1,0:T(4,128)S(1)}, u32[]{:S(2)}, u32[]{:S(2)}) collective-permute-start(f32[4,512]{1,0:T(4,128)S(1)} %get-tuple-element.310), channel_id=1, source_target_pairs={{1,0},{3,2},{5,4},{7,6},{9,8},{11,10},{13,12},{15,14},{17,16},{19,... | collective-permute-start | bytes 24584 | tf_op jit(solution)/shard_map/while/body/eval_jaxpr/ppermute | solution.py:31
  99.3 3.8 %collective-permute-start = (f32[4,512]{1,0:T(4,128)S(1)}, f32[4,512]{1,0:T(4,128)S(1)}, u32[]{:S(2)}, u32[]{:S(2)}) collective-permute-start(f32[4,512]{1,0:T(4,128)S(1)} %get-tuple-element.309), channel_id=1, source_target_pairs={{0,1},{2,3},{4,5},{6,7},{8,9},{10,11},{12,13},{14,15},{16,17},{18,... | collective-permute-start | bytes 24584 | tf_op jit(solution)/shard_map/while/body/eval_jaxpr/ppermute | solution.py:29
  103.4 4.4 %collective-permute-start.1 = (f32[4,512]{1,0:T(4,128)S(1)}, f32[4,512]{1,0:T(4,128)S(1)}, u32[]{:S(2)}, u32[]{:S(2)}) collective-permute-start(f32[4,512]{1,0:T(4,128)S(1)} %get-tuple-element.310), channel_id=1, source_target_pairs={{1,0},{3,2},{5,4},{7,6},{9,8},{11,10},{13,12},{15,14},{17,16},{19,... | collective-permute-start | bytes 24584 | tf_op jit(solution)/shard_map/while/body/eval_jaxpr/ppermute | solution.py:31
  104.7 3.8 %collective-permute-start = (f32[4,512]{1,0:T(4,128)S(1)}, f32[4,512]{1,0:T(4,128)S(1)}, u32[]{:S(2)}, u32[]{:S(2)}) collective-permute-start(f32[4,512]{1,0:T(4,128)S(1)} %get-tuple-element.309), channel_id=1, source_target_pairs={{0,1},{2,3},{4,5},{6,7},{8,9},{10,11},{12,13},{14,15},{16,17},{18,... | collective-permute-start | bytes 24584 | tf_op jit(solution)/shard_map/while/body/eval_jaxpr/ppermute | solution.py:29
  108.9 4.4 %collective-permute-start.1 = (f32[4,512]{1,0:T(4,128)S(1)}, f32[4,512]{1,0:T(4,128)S(1)}, u32[]{:S(2)}, u32[]{:S(2)}) collective-permute-start(f32[4,512]{1,0:T(4,128)S(1)} %get-tuple-element.310), channel_id=1, source_target_pairs={{1,0},{3,2},{5,4},{7,6},{9,8},{11,10},{13,12},{15,14},{17,16},{19,... | collective-permute-start | bytes 24584 | tf_op jit(solution)/shard_map/while/body/eval_jaxpr/ppermute | solution.py:31
  110.2 3.8 %collective-permute-start = (f32[4,512]{1,0:T(4,128)S(1)}, f32[4,512]{1,0:T(4,128)S(1)}, u32[]{:S(2)}, u32[]{:S(2)}) collective-permute-start(f32[4,512]{1,0:T(4,128)S(1)} %get-tuple-element.309), channel_id=1, source_target_pairs={{0,1},{2,3},{4,5},{6,7},{8,9},{10,11},{12,13},{14,15},{16,17},{18,... | collective-permute-start | bytes 24584 | tf_op jit(solution)/shard_map/while/body/eval_jaxpr/ppermute | solution.py:29
  114.3 4.4 %collective-permute-start.1 = (f32[4,512]{1,0:T(4,128)S(1)}, f32[4,512]{1,0:T(4,128)S(1)}, u32[]{:S(2)}, u32[]{:S(2)}) collective-permute-start(f32[4,512]{1,0:T(4,128)S(1)} %get-tuple-element.310), channel_id=1, source_target_pairs={{1,0},{3,2},{5,4},{7,6},{9,8},{11,10},{13,12},{15,14},{17,16},{19,... | collective-permute-start | bytes 24584 | tf_op jit(solution)/shard_map/while/body/eval_jaxpr/ppermute | solution.py:31
  119.7 4.4 %collective-permute-start.1 = (f32[4,512]{1,0:T(4,128)S(1)}, f32[4,512]{1,0:T(4,128)S(1)}, u32[]{:S(2)}, u32[]{:S(2)}) collective-permute-start(f32[4,512]{1,0:T(4,128)S(1)} %get-tuple-element.310), channel_id=1, source_target_pairs={{1,0},{3,2},{5,4},{7,6},{9,8},{11,10},{13,12},{15,14},{17,16},{19,... | collective-permute-start | bytes 24584 | tf_op jit(solution)/shard_map/while/body/eval_jaxpr/ppermute | solution.py:31
  125.1 4.4 %collective-permute-start.1 = (f32[4,512]{1,0:T(4,128)S(1)}, f32[4,512]{1,0:T(4,128)S(1)}, u32[]{:S(2)}, u32[]{:S(2)}) collective-permute-start(f32[4,512]{1,0:T(4,128)S(1)} %get-tuple-element.310), channel_id=1, source_target_pairs={{1,0},{3,2},{5,4},{7,6},{9,8},{11,10},{13,12},{15,14},{17,16},{19,... | collective-permute-start | bytes 24584 | tf_op jit(solution)/shard_map/while/body/eval_jaxpr/ppermute | solution.py:31
  130.5 4.4 %collective-permute-start.1 = (f32[4,512]{1,0:T(4,128)S(1)}, f32[4,512]{1,0:T(4,128)S(1)}, u32[]{:S(2)}, u32[]{:S(2)}) collective-permute-start(f32[4,512]{1,0:T(4,128)S(1)} %get-tuple-element.310), channel_id=1, source_target_pairs={{1,0},{3,2},{5,4},{7,6},{9,8},{11,10},{13,12},{15,14},{17,16},{19,... | collective-permute-start | bytes 24584 | tf_op jit(solution)/shard_map/while/body/eval_jaxpr/ppermute | solution.py:31
  135.9 4.4 %collective-permute-start.1 = (f32[4,512]{1,0:T(4,128)S(1)}, f32[4,512]{1,0:T(4,128)S(1)}, u32[]{:S(2)}, u32[]{:S(2)}) collective-permute-start(f32[4,512]{1,0:T(4,128)S(1)} %get-tuple-element.310), channel_id=1, source_target_pairs={{1,0},{3,2},{5,4},{7,6},{9,8},{11,10},{13,12},{15,14},{17,16},{19,... | collective-permute-start | bytes 24584 | tf_op jit(solution)/shard_map/while/body/eval_jaxpr/ppermute | solution.py:31
  141.4 4.4 %collective-permute-start.1 = (f32[4,512]{1,0:T(4,128)S(1)}, f32[4,512]{1,0:T(4,128)S(1)}, u32[]{:S(2)}, u32[]{:S(2)}) collective-permute-start(f32[4,512]{1,0:T(4,128)S(1)} %get-tuple-element.310), channel_id=1, source_target_pairs={{1,0},{3,2},{5,4},{7,6},{9,8},{11,10},{13,12},{15,14},{17,16},{19,... | collective-permute-start | bytes 24584 | tf_op jit(solution)/shard_map/while/body/eval_jaxpr/ppermute | solution.py:31
  146.8 4.4 %collective-permute-start.1 = (f32[4,512]{1,0:T(4,128)S(1)}, f32[4,512]{1,0:T(4,128)S(1)}, u32[]{:S(2)}, u32[]{:S(2)}) collective-permute-start(f32[4,512]{1,0:T(4,128)S(1)} %get-tuple-element.310), channel_id=1, source_target_pairs={{1,0},{3,2},{5,4},{7,6},{9,8},{11,10},{13,12},{15,14},{17,16},{19,... | collective-permute-start | bytes 24584 | tf_op jit(solution)/shard_map/while/body/eval_jaxpr/ppermute | solution.py:31
  152.2 4.4 %collective-permute-start.1 = (f32[4,512]{1,0:T(4,128)S(1)}, f32[4,512]{1,0:T(4,128)S(1)}, u32[]{:S(2)}, u32[]{:S(2)}) collective-permute-start(f32[4,512]{1,0:T(4,128)S(1)} %get-tuple-element.310), channel_id=1, source_target_pairs={{1,0},{3,2},{5,4},{7,6},{9,8},{11,10},{13,12},{15,14},{17,16},{19,... | collective-permute-start | bytes 24584 | tf_op jit(solution)/shard_map/while/body/eval_jaxpr/ppermute | solution.py:31
  157.6 4.4 %collective-permute-start.1 = (f32[4,512]{1,0:T(4,128)S(1)}, f32[4,512]{1,0:T(4,128)S(1)}, u32[]{:S(2)}, u32[]{:S(2)}) collective-permute-start(f32[4,512]{1,0:T(4,128)S(1)} %get-tuple-element.310), channel_id=1, source_target_pairs={{1,0},{3,2},{5,4},{7,6},{9,8},{11,10},{13,12},{15,14},{17,16},{19,... | collective-permute-start | bytes 24584 | tf_op jit(solution)/shard_map/while/body/eval_jaxpr/ppermute | solution.py:31
  163.0 4.4 %collective-permute-start.1 = (f32[4,512]{1,0:T(4,128)S(1)}, f32[4,512]{1,0:T(4,128)S(1)}, u32[]{:S(2)}, u32[]{:S(2)}) collective-permute-start(f32[4,512]{1,0:T(4,128)S(1)} %get-tuple-element.310), channel_id=1, source_target_pairs={{1,0},{3,2},{5,4},{7,6},{9,8},{11,10},{13,12},{15,14},{17,16},{19,... | collective-permute-start | bytes 24584 | tf_op jit(solution)/shard_map/while/body/eval_jaxpr/ppermute | solution.py:31
  168.4 4.4 %collective-permute-start.1 = (f32[4,512]{1,0:T(4,128)S(1)}, f32[4,512]{1,0:T(4,128)S(1)}, u32[]{:S(2)}, u32[]{:S(2)}) collective-permute-start(f32[4,512]{1,0:T(4,128)S(1)} %get-tuple-element.310), channel_id=1, source_target_pairs={{1,0},{3,2},{5,4},{7,6},{9,8},{11,10},{13,12},{15,14},{17,16},{19,... | collective-permute-start | bytes 24584 | tf_op jit(solution)/shard_map/while/body/eval_jaxpr/ppermute | solution.py:31
  173.9 4.4 %collective-permute-start.1 = (f32[4,512]{1,0:T(4,128)S(1)}, f32[4,512]{1,0:T(4,128)S(1)}, u32[]{:S(2)}, u32[]{:S(2)}) collective-permute-start(f32[4,512]{1,0:T(4,128)S(1)} %get-tuple-element.310), channel_id=1, source_target_pairs={{1,0},{3,2},{5,4},{7,6},{9,8},{11,10},{13,12},{15,14},{17,16},{19,... | collective-permute-start | bytes 24584 | tf_op jit(solution)/shard_map/while/body/eval_jaxpr/ppermute | solution.py:31
  179.3 4.4 %collective-permute-start.1 = (f32[4,512]{1,0:T(4,128)S(1)}, f32[4,512]{1,0:T(4,128)S(1)}, u32[]{:S(2)}, u32[]{:S(2)}) collective-permute-start(f32[4,512]{1,0:T(4,128)S(1)} %get-tuple-element.310), channel_id=1, source_target_pairs={{1,0},{3,2},{5,4},{7,6},{9,8},{11,10},{13,12},{15,14},{17,16},{19,... | collective-permute-start | bytes 24584 | tf_op jit(solution)/shard_map/while/body/eval_jaxpr/ppermute | solution.py:31
  184.7 4.4 %collective-permute-start.1 = (f32[4,512]{1,0:T(4,128)S(1)}, f32[4,512]{1,0:T(4,128)S(1)}, u32[]{:S(2)}, u32[]{:S(2)}) collective-permute-start(f32[4,512]{1,0:T(4,128)S(1)} %get-tuple-element.310), channel_id=1, source_target_pairs={{1,0},{3,2},{5,4},{7,6},{9,8},{11,10},{13,12},{15,14},{17,16},{19,... | collective-permute-start | bytes 24584 | tf_op jit(solution)/shard_map/while/body/eval_jaxpr/ppermute | solution.py:31
  190.1 4.4 %collective-permute-start.1 = (f32[4,512]{1,0:T(4,128)S(1)}, f32[4,512]{1,0:T(4,128)S(1)}, u32[]{:S(2)}, u32[]{:S(2)}) collective-permute-start(f32[4,512]{1,0:T(4,128)S(1)} %get-tuple-element.310), channel_id=1, source_target_pairs={{1,0},{3,2},{5,4},{7,6},{9,8},{11,10},{13,12},{15,14},{17,16},{19,... | collective-permute-start | bytes 24584 | tf_op jit(solution)/shard_map/while/body/eval_jaxpr/ppermute | solution.py:31
  195.5 4.4 %collective-permute-start.1 = (f32[4,512]{1,0:T(4,128)S(1)}, f32[4,512]{1,0:T(4,128)S(1)}, u32[]{:S(2)}, u32[]{:S(2)}) collective-permute-start(f32[4,512]{1,0:T(4,128)S(1)} %get-tuple-element.310), channel_id=1, source_target_pairs={{1,0},{3,2},{5,4},{7,6},{9,8},{11,10},{13,12},{15,14},{17,16},{19,... | collective-permute-start | bytes 24584 | tf_op jit(solution)/shard_map/while/body/eval_jaxpr/ppermute | solution.py:31
  200.9 4.4 %collective-permute-start.1 = (f32[4,512]{1,0:T(4,128)S(1)}, f32[4,512]{1,0:T(4,128)S(1)}, u32[]{:S(2)}, u32[]{:S(2)}) collective-permute-start(f32[4,512]{1,0:T(4,128)S(1)} %get-tuple-element.310), channel_id=1, source_target_pairs={{1,0},{3,2},{5,4},{7,6},{9,8},{11,10},{13,12},{15,14},{17,16},{19,... | collective-permute-start | bytes 24584 | tf_op jit(solution)/shard_map/while/body/eval_jaxpr/ppermute | solution.py:31
  (22 other events, 142.3 us)
where the time goes:
time: 208 us; the launch traced here: 207 us
  starting transfers between devices  116 us (56%)
  blocking collectives  31.3 us (15%)
  waiting for transfers between devices  24.1 us (12%)
  other arithmetic  15.9 us (8%)
  local copies, waits for them, and re-layouts  14.2 us (7%)
  loops' own time  3.08 us (1%)
    ppermute x24, starting transfers between devices, extended(): lax.ppermute(tail, axis, [(i, (i + 1) % count) for i in range(ends)])  72.6 us
    all_gather x1, blocking collectives, local(): panel_part = lax.all_gather(velocity, 'shot', axis=1, tiled=True)  31.3 us
    ppermute x24, starting transfers between devices, extended(): lax.ppermute(head, axis, [((i + 1) % count, i) for i in range(ends)])  31 us
    ppermute x24, waiting for transfers between devices, extended(): lax.ppermute(tail, axis, [(i, (i + 1) % count) for i in range(ends)])  17.3 us
    all_to_all x1, starting transfers between devices, local(): lax.all_to_all(node_buffer, 'shot', split_axis=0, concat_axis=0, tiled=True)  7.25 us
    scatter-add x1, other arithmetic, local(): jnp.zeros((STEPS, depth_rows * width_cols), jnp.float32).at[:, node_rows]  7.07 us
    unnamed x11, local copies, waits for them, and re-layouts  6.9 us
    all_to_all x1, waiting for transfers between devices, local(): lax.all_to_all(trace_buffer, 'shot', split_axis=0, concat_axis=0, tiled=T...  6.8 us
  transfers between devices with their start and end apart: 50, of which 25 were waited for; matrix products, arithmetic and copies ran while one was open for 3% of the time, Pallas kernels for 0%

commit v1 on v0

v1 whole, which is shorter than its diff:
```python
import math

import jax
import jax.numpy as jnp
import numpy as np
from jax import lax
from jax.experimental import pallas as pl
from jax.experimental.pallas import tpu as pltpu
from jax.sharding import PartitionSpec as P

NS = 256
STEPS = 24
CAP = 64
LANES = 128
SUB = 8
ROWS = 32

LAP_CENTER = -205.0 / 72.0
LAP_TAPS = (1.6, -0.2, 8.0 / 315.0, -1.0 / 560.0)
PEAK = 0.12
DELAY = 5.0
SOURCE_GAIN = 2.0
RATIO = 0.1
NT = (((1,), (1,)), ((), ()))


def dot_nt(a, b):
    return lax.dot_general(a, b, NT, preferred_element_type=jnp.float32)


def split_table():
    k = np.arange(NS, dtype=np.float64)[:, None] + 0.5
    t = np.arange(STEPS, dtype=np.float64)[None, :] + 1.0
    table = np.cos(math.pi * k * t / NS) * math.sqrt(2.0 / NS)
    rest = np.zeros((ROWS, NS), np.float32)
    rest[:STEPS] = table.T
    parts = []
    for _ in range(3):
        part = rest.astype(jnp.bfloat16)
        parts.append(part)
        rest = rest - part.astype(np.float32)
    return jnp.asarray(np.concatenate(parts, axis=0))


def ricker_value(step):
    a = (math.pi * PEAK * (step - DELAY)) ** 2
    return SOURCE_GAIN * (1.0 - 2.0 * a) * math.exp(-a)


def exchange_kernel(
    shots, slabs, table_ref, now_ref, before_ref, velocity_ref, traces_ref, shot_ref, node_ref,
    gathered, fields, message, own, send_sem, recv_sem, field_send, field_recv,
):
    peers = shots * slabs
    shot, slab = lax.axis_index("shot"), lax.axis_index("slab")
    me = shot * slabs + slab
    depth, width = now_ref.shape
    groups = depth // SUB
    rows = traces_ref.shape[0]

    def place(d):
        index = lax.rem(me + d, peers)
        return index // slabs, lax.rem(index, slabs)

    barrier = pltpu.get_barrier_semaphore()

    def greet(d, carry):
        to_shot, to_slab = place(d)
        pl.semaphore_signal(
            barrier, inc=1, device_id={"shot": to_shot, "slab": to_slab},
            device_id_type=pl.DeviceIdType.MESH,
        )
        return carry

    lax.fori_loop(1, peers, greet, 0)

    for r in range(depth):
        to = (r % groups) * SUB + r // groups
        own[0, to : to + 1, :] = now_ref[r : r + 1, :]
        own[1, to : to + 1, :] = before_ref[r : r + 1, :]

    parts = dot_nt(table_ref[...], traces_ref[...])
    amplitude = parts[0:ROWS] + parts[ROWS : 2 * ROWS] + parts[2 * ROWS : 3 * ROWS]
    node = node_ref[...]
    lateral = node % width
    row = lax.broadcasted_iota(jnp.int32, (ROWS, rows), 0)
    where_to = jnp.where(
        row == STEPS, node // width, jnp.where(row == STEPS + 1, lateral // 256, lateral % 256)
    ).astype(jnp.float32)
    high = jnp.where(row < STEPS, amplitude, where_to).astype(jnp.bfloat16)
    low = jnp.where(row < STEPS, amplitude - high.astype(jnp.float32), where_to).astype(
        jnp.bfloat16
    )
    target = shot_ref[...]
    chosen = lax.broadcasted_iota(jnp.int32, (shots, rows), 0) == target
    onehot = jnp.where(chosen, 1.0, 0.0)
    ahead = jnp.where(
        lax.broadcasted_iota(jnp.int32, (rows, rows), 0)
        < lax.broadcasted_iota(jnp.int32, (rows, rows), 1),
        1.0, 0.0,
    ).astype(jnp.bfloat16)
    count = jnp.dot(onehot.astype(jnp.bfloat16), ahead, preferred_element_type=jnp.float32)
    position = jnp.sum(onehot * count, axis=0, keepdims=True)
    slot = lax.broadcasted_iota(jnp.int32, (LANES, rows), 0).astype(jnp.float32)

    turn = lax.broadcasted_iota(jnp.int32, (depth, depth), 0)
    turned = jnp.where(
        (turn % SUB) * groups + turn // SUB
        == lax.broadcasted_iota(jnp.int32, (depth, depth), 1),
        1.0, 0.0,
    ).astype(jnp.bfloat16)
    panel = jnp.dot(turned, velocity_ref[...], preferred_element_type=jnp.float32).astype(
        jnp.bfloat16
    )

    def fill(s, carry):
        mine = target == s
        to_high = jnp.where(mine, position, -1.0)
        to_low = jnp.where(mine, position + float(CAP), -1.0)
        pick_high = jnp.where(slot == to_high, 1.0, 0.0).astype(jnp.bfloat16)
        pick_low = jnp.where(slot == to_low, 1.0, 0.0).astype(jnp.bfloat16)
        message[s, 0] = (dot_nt(high, pick_high) + dot_nt(low, pick_low)).astype(jnp.bfloat16)
        message[s, 1] = panel
        return carry

    lax.fori_loop(0, shots, fill, 0, unroll=shots <= 8)

    pl.semaphore_wait(barrier, peers - 1)

    def field_copy(d):
        return pltpu.make_async_remote_copy(
            src_ref=own, dst_ref=fields.at[slab],
            send_sem=field_send.at[d], recv_sem=field_recv.at[d],
            device_id={"slab": lax.rem(slab + d, slabs)},
            device_id_type=pl.DeviceIdType.MESH,
        )

    def message_copy(d):
        to_shot, to_slab = place(d)
        return pltpu.make_async_remote_copy(
            src_ref=message.at[to_shot], dst_ref=gathered.at[slab, shot],
            send_sem=send_sem.at[d], recv_sem=recv_sem.at[d],
            device_id={"shot": to_shot, "slab": to_slab},
            device_id_type=pl.DeviceIdType.MESH,
        )

    def start_message(d, carry):
        message_copy(d).start()
        return carry

    def start_field(d, carry):
        field_copy(d).start()
        return carry

    def wait_message(d, carry):
        message_copy(d).wait()
        return carry

    def wait_field(d, carry):
        field_copy(d).wait()
        return carry

    lax.fori_loop(1, peers, start_message, 0)
    lax.fori_loop(1, slabs, start_field, 0)
    gathered[slab, shot] = message[shot]
    fields[slab] = own[...]
    lax.fori_loop(1, slabs, wait_field, 0)
    lax.fori_loop(1, peers, wait_message, 0)


def wave_kernel(
    shots, slabs, offset_ref, source_ref, gathered, fields, out_ref,
    injection, left, right, courant, first, second,
):
    depth, width = out_ref.shape
    groups = depth // SUB
    columns = width // LANES
    slab = lax.axis_index("slab")
    few = slabs <= 2

    lane = lax.broadcasted_iota(jnp.int32, (SUB, LANES), 1)
    sub = lax.broadcasted_iota(jnp.int32, (SUB, LANES), 0)
    offset = offset_ref[0]
    panel0 = offset // LANES
    shift = offset % LANES
    keep = lax.broadcasted_iota(jnp.int32, (depth, LANES), 1) < LANES - shift
    at_row = lax.broadcasted_iota(jnp.int32, (depth, LANES), 0)
    row_depth = ((at_row % SUB) * groups + at_row // SUB).astype(jnp.float32)
    at_cell = lax.broadcasted_iota(jnp.int32, (width, LANES), 0).astype(jnp.float32)

    def prepare(j, carry):
        turned = []
        for c in range(columns + 1):
            panel = jnp.minimum(panel0 + c, shots - 1)
            turned.append(
                pltpu.roll(
                    gathered[j, panel, 1].astype(jnp.float32), lax.rem(LANES - shift, LANES), 1
                )
            )
        for c in range(columns):
            window = jnp.where(keep, turned[c], turned[c + 1]) * RATIO
            courant[j, :, c * LANES : (c + 1) * LANES] = window * window

        def source(s, inner):
            lanes = pl.ds(pl.multiple_of(s * LANES, LANES), LANES)
            values = gathered[j, s, 0].astype(jnp.float32)
            at_depth = values[STEPS : STEPS + 1]
            at_lateral = values[STEPS + 1 : STEPS + 2] * 256.0 + values[STEPS + 2 : STEPS + 3]
            chosen = row_depth == at_depth
            for t in range(STEPS):
                left[t * depth : (t + 1) * depth, lanes] = jnp.where(
                    chosen, values[t : t + 1], 0.0
                ).astype(jnp.bfloat16)
            right[:, lanes] = jnp.where(at_cell == at_lateral, 1.0, 0.0).astype(jnp.bfloat16)
            return inner

        lax.fori_loop(0, shots, source, 0, unroll=shots <= 8)
        injection[j] = dot_nt(left[...], right[...])
        first[j] = fields[j, 0]
        second[j] = fields[j, 1]
        return carry

    lax.fori_loop(0, slabs, prepare, 0, unroll=few)

    source = source_ref[0]
    source_depth = source // width
    source_slab = source_depth // depth
    within = source_depth % depth
    source_row = (within % groups) * SUB + within // groups
    here = lax.broadcasted_iota(jnp.int32, (1, width), 1) == source % width
    for t in range(STEPS):
        spot = pl.ds(t * depth + source_row, 1)
        injection[source_slab, spot, :] = injection[source_slab, spot, :] + jnp.where(
            here, ricker_value(float(t)), 0.0
        )

    def step(t, now, other):
        def one_slab(j, carry):
            def cell(jj, v, c):
                return now[jj, v * SUB : (v + 1) * SUB, c * LANES : (c + 1) * LANES]

            up_ok = jnp.where(j + 1 < slabs, 1.0, 0.0) if not few else None
            down_ok = jnp.where(j > 0, 1.0, 0.0) if not few else None

            def ups(v, c):
                base = pltpu.roll(cell(j, v, c), SUB - 1, 0)
                if few:
                    beyond = pltpu.roll(cell(j + 1, v, c), SUB - 1, 0) if j + 1 < slabs else 0.0
                else:
                    beyond = pltpu.roll(cell(jnp.minimum(j + 1, slabs - 1), v, c), SUB - 1, 0)
                    beyond = beyond * up_ok
                return jnp.where(sub == SUB - 1, beyond, base)

            def downs(v, c):
                base = pltpu.roll(cell(j, v, c), 1, 0)
                if few:
                    beyond = pltpu.roll(cell(j - 1, v, c), 1, 0) if j > 0 else 0.0
                else:
                    beyond = pltpu.roll(cell(jnp.maximum(j - 1, 0), v, c), 1, 0) * down_ok
                return jnp.where(sub == 0, beyond, base)

            up = [[ups(v, c) for c in range(columns)] for v in range(groups)]
            down = [[downs(v, c) for c in range(columns)] for v in range(groups)]
            for v in range(groups):
                line = [cell(j, v, c) for c in range(columns)]
                totals = [LAP_CENTER * 2.0 * line[c] for c in range(columns)]
                for k in range(1, 5):
                    plus = [pltpu.roll(line[c], LANES - k, 1) for c in range(columns)]
                    minus = [pltpu.roll(line[c], k, 1) for c in range(columns)]
                    for c in range(columns):
                        after = plus[c + 1] if c + 1 < columns else 0.0
                        prior = minus[c - 1] if c > 0 else 0.0
                        sides = jnp.where(lane < LANES - k, plus[c], after) + jnp.where(
                            lane < k, prior, minus[c]
                        )
                        below = cell(j, v + k, c) if v + k < groups else up[v + k - groups][c]
                        above = cell(j, v - k, c) if v >= k else down[v - k + groups][c]
                        totals[c] = totals[c] + LAP_TAPS[k - 1] * (sides + (below + above))
                for c in range(columns):
                    rows = slice(v * SUB, (v + 1) * SUB)
                    lanes = slice(c * LANES, (c + 1) * LANES)
                    start = pl.multiple_of(t * depth + v * SUB, SUB)
                    other[j, rows, lanes] = (
                        2.0 * line[c]
                        - other[j, rows, lanes]
                        + courant[j, rows, lanes] * totals[c]
                        + injection[j, pl.ds(start, SUB), lanes]
                    )
            return carry

        if few:
            for j in range(slabs):
                one_slab(j, 0)
        else:
            lax.fori_loop(0, slabs, one_slab, 0)

    def pair(i, carry):
        step(2 * i, first, second)
        step(2 * i + 1, second, first)
        return carry

    lax.fori_loop(0, STEPS // 2, pair, 0)
    for r in range(depth):
        at = (r % groups) * SUB + r // groups
        out_ref[r : r + 1, :] = first[slab, at : at + 1, :]


def local(
    field_now, field_before, velocity, offsets, source_cell, traces, trace_shot, trace_node_cell
):
    depth, width = field_now.shape
    shots, slabs = lax.axis_size("shot"), lax.axis_size("slab")
    rows = traces.shape[1]
    vmem = pl.BlockSpec(memory_space=pltpu.VMEM)
    smem = pl.BlockSpec(memory_space=pltpu.SMEM)
    def exchange(*refs):
        exchange_kernel(shots, slabs, *refs)

    def wave(*refs):
        wave_kernel(shots, slabs, *refs)

    gathered, fields = pl.pallas_call(
        exchange,
        out_shape=(
            jax.ShapeDtypeStruct((slabs, shots, 2, depth, LANES), jnp.bfloat16),
            jax.ShapeDtypeStruct((slabs, 2, depth, width), jnp.float32),
        ),
        in_specs=[vmem] * 7,
        out_specs=(vmem, vmem),
        scratch_shapes=[
            pltpu.VMEM((shots, 2, depth, LANES), jnp.bfloat16),
            pltpu.VMEM((2, depth, width), jnp.float32),
            pltpu.SemaphoreType.DMA((shots * slabs,)),
            pltpu.SemaphoreType.DMA((shots * slabs,)),
            pltpu.SemaphoreType.DMA((slabs,)),
            pltpu.SemaphoreType.DMA((slabs,)),
        ],
        compiler_params=pltpu.CompilerParams(
            collective_id=0, has_side_effects=True, vmem_limit_bytes=48 << 20
        ),
    )(
        split_table(), field_now, field_before, velocity, traces[0],
        trace_shot.reshape(1, rows), trace_node_cell,
    )
    return pl.pallas_call(
        wave,
        out_shape=jax.ShapeDtypeStruct((depth, width), jnp.float32),
        in_specs=[smem, smem, vmem, vmem],
        out_specs=vmem,
        scratch_shapes=[
            pltpu.VMEM((slabs, STEPS * depth, width), jnp.float32),
            pltpu.VMEM((STEPS * depth, shots * LANES), jnp.bfloat16),
            pltpu.VMEM((width, shots * LANES), jnp.bfloat16),
            pltpu.VMEM((slabs, depth, width), jnp.float32),
            pltpu.VMEM((slabs, depth, width), jnp.float32),
            pltpu.VMEM((slabs, depth, width), jnp.float32),
        ],
        compiler_params=pltpu.CompilerParams(vmem_limit_bytes=48 << 20),
    )(offsets, source_cell, gathered, fields)


def solution(mesh):
    in_specs = (
        P("slab", ("groups", "shot")),
        P("slab", ("groups", "shot")),
        P("slab", ("groups", "shot")),
        P(("groups", "shot")),
        P(("groups", "shot")),
        P("slab", ("groups", "shot"), None),
        P("slab", ("groups", "shot"), None),
        P("slab", ("groups", "shot")),
    )
    out_specs = P("slab", ("groups", "shot"))
    return jax.shard_map(local, mesh=mesh, in_specs=in_specs, out_specs=out_specs, check_vma=False)
```

time: 208 us -> 28.1 us (0.14)
  starting transfers between devices: 116 us -> 0 us
  blocking collectives: 31.3 us -> 0 us
  waiting for transfers between devices: 24.1 us -> 0 us
  Pallas kernels: 0 us -> 21.7 us
  other arithmetic: 15.9 us -> 0 us
  local copies, waits for them, and re-layouts: 14.2 us -> 4.76 us
  loops' own time: 3.08 us -> 0 us
    ppermute x48 -> x0, starting transfers between devices: 104 us -> none  [the longest x24 72.6 us: extended(): lax.ppermute(tail, axis, [(i, (i + 1) % count) for i in range(ends)])]
    all_gather x1 -> x0, blocking collectives: 31.3 us -> none  [local(): panel_part = lax.all_gather(velocity, 'shot', axis=1, tiled=True)]
    pallas_call x0 -> x2, Pallas kernels: none -> 21.7 us  [the longest x1 11.1 us: local(): pl.pallas_call(exchange, out_shape=(jax.ShapeDtypeStruct((slabs, shots, 2...]
    ppermute x48 -> x0, waiting for transfers between devices: 17.3 us -> none  [the longest x24 17.3 us: extended(): lax.ppermute(tail, axis, [(i, (i + 1) % count) for i in range(ends)])]
    all_to_all x2 -> x0, starting transfers between devices: 12.7 us -> none  [the longest x1 7.25 us: local(): lax.all_to_all(node_buffer, 'shot', split_axis=0, concat_axis=0, tiled=True)]
    scatter-add x1 -> x0, other arithmetic: 7.07 us -> none  [local(): jnp.zeros((STEPS, depth_rows * width_cols), jnp.float32).at[:, node_rows]]
    all_to_all x2 -> x0, waiting for transfers between devices: 6.8 us -> none  [the longest x1 6.8 us: local(): lax.all_to_all(trace_buffer, 'shot', split_axis=0, concat_axis=0, tiled=T...]
    add x25 -> x0, other arithmetic: 5.11 us -> none  [the longest x24 5.1 us: advance(): 2.0 * present - earlier + courant * laplace(depth_padded, present)]
  transfers between devices with their start and end apart: 50 -> 0, of which waited for: 25 -> 0; matrix products, arithmetic and copies ran while one was open for 3% -> 0% of each run, Pallas kernels for 0% -> 0%
where the time goes in v1:
time: 28.1 us; the launch traced here: 27.8 us
  Pallas kernels  21.7 us (77%)
  local copies, waits for them, and re-layouts  4.76 us (17%)
  between operations  1.33 us (5%)
    pallas_call x1, Pallas kernels, local(): pl.pallas_call(exchange, out_shape=(jax.ShapeDtypeStruct((slabs, shots, 2...  11.1 us
    pallas_call x1, Pallas kernels, local(): pl.pallas_call(wave, out_shape=jax.ShapeDtypeStruct((depth, width), jnp.f...  10.6 us
    unnamed x14, local copies, waits for them, and re-layouts  4.76 us

profile of v1, /device:TPU:0, one launch (start us, length us, event | category | flops | bytes accessed | tf_op | source)
XLA Modules:
  0.0 27.8 jit_solution(1357921738939197848)
XLA Ops:
  1.3 0.0 copy-start.6
  1.3 0.0 copy-start.5
  1.3 0.7 %copy-done.6 = s32[1,256]{1,0:T(1,128)S(1)} copy-done((s32[1,256]{1,0:T(1,128)S(1)}, s32[1,256]{1,0:T(1,128)}, u32[]{:S(2)}) %copy-start.6) | copy-done | bytes 1048
  2.0 0.0 copy-done.5
  2.0 0.0 copy-start
  2.0 0.9 %copy-done = bf16[1,256,256]{2,1,0:T(8,128)(2,1)S(1)} copy-done((bf16[1,256,256]{2,1,0:T(8,128)(2,1)S(1)}, bf16[1,256,256]{2,1,0:T(8,128)(2,1)}, u32[]{:S(2)}) %copy-start) | copy-done | bytes 131096
  2.9 0.0 copy-start.1
  2.9 0.8 %copy-done.1 = f32[32,512]{1,0:T(8,128)S(1)} copy-done((f32[32,512]{1,0:T(8,128)S(1)}, f32[32,512]{1,0:T(8,128)}, u32[]{:S(2)}) %copy-start.1) | copy-done | bytes 65560
  3.7 0.0 copy-start.2
  3.7 0.8 %copy-done.2 = f32[32,512]{1,0:T(8,128)S(1)} copy-done((f32[32,512]{1,0:T(8,128)S(1)}, f32[32,512]{1,0:T(8,128)}, u32[]{:S(2)}) %copy-start.2) | copy-done | bytes 65560
  4.6 0.0 copy-start.3
  4.6 0.8 %copy-done.3 = bf16[96,256]{1,0:T(8,128)(2,1)S(1)} copy-done((bf16[96,256]{1,0:T(8,128)(2,1)S(1)}, bf16[96,256]{1,0:T(8,128)(2,1)}, u32[]{:S(2)}) %copy-start.3) | copy-done | bytes 49176
  5.4 0.0 copy-start.4
  5.4 0.7 %copy-done.4 = bf16[32,128]{1,0:T(8,128)(2,1)S(1)} copy-done((bf16[32,128]{1,0:T(8,128)(2,1)S(1)}, bf16[32,128]{1,0:T(8,128)(2,1)}, u32[]{:S(2)}) %copy-start.4) | copy-done | bytes 8216
  6.1 11.1 %shard_map.91 = (bf16[2,8,2,32,128]{4,3,2,1,0:T(8,128)(2,1)S(1)}, f32[2,2,32,512]{3,2,1,0:T(8,128)S(1)}) custom-call(bf16[96,256]{1,0:T(8,128)(2,1)S(1)} %copy-done.3, f32[32,512]{1,0:T(8,128)S(1)} %copy-done.1, f32[32,512]{1,0:T(8,128)S(1)} %copy-done.2, bf16[32,128]{1,0:T(8,128)(2,1)S(1)} %copy-done.4, bf16[256,256]{1,0:T(8,128)(2,1)S(1)} %bitcast.2, ...), custom_call_target="tpu_custom_call" | custom-call | tf_op jit(solution)/shard_map/pallas_call | solution.py:322
  17.2 10.6 %shard_map.92 = f32[32,512]{1,0:T(8,128)} custom-call(s32[1]{0:T(128)S(6)} %copy.10.refs_0_, s32[1]{0:T(128)S(6)} %copy.11.refs_1_, bf16[2,8,2,32,128]{4,3,2,1,0:T(8,128)(2,1)S(1)} %get-tuple-element.7.refs_2_, f32[2,2,32,512]{3,2,1,0:T(8,128)S(1)} %get-tuple-element.8.refs_3_), custom_call_target="tpu_custom_call" | custom-call | tf_op jit(solution)/shard_map/pallas_call | solution.py:345
Async XLA Ops:
  1.3 0.7 %copy-start.6 = (s32[1,256]{1,0:T(1,128)S(1)}, s32[1,256]{1,0:T(1,128)}, u32[]{:S(2)}) copy-start(s32[1,256]{1,0:T(1,128)} %refs_6_.1) | copy-start | bytes 3076
  1.3 0.7 %copy-start.5 = (s32[1,256,1]{1,2,0:T(1,128)S(1)}, s32[1,256,1]{1,2,0:T(1,128)}, u32[]{:S(2)}) copy-start(s32[1,256,1]{1,2,0:T(1,128)} %param.15) | copy-start | bytes 3076
  2.0 0.9 %copy-start = (bf16[1,256,256]{2,1,0:T(8,128)(2,1)S(1)}, bf16[1,256,256]{2,1,0:T(8,128)(2,1)}, u32[]{:S(2)}) copy-start(bf16[1,256,256]{2,1,0:T(8,128)(2,1)} %param.14) | copy-start | bytes 393220
  2.9 0.8 %copy-start.1 = (f32[32,512]{1,0:T(8,128)S(1)}, f32[32,512]{1,0:T(8,128)}, u32[]{:S(2)}) copy-start(f32[32,512]{1,0:T(8,128)} %refs_1_.2) | copy-start | bytes 196612
  3.7 0.8 %copy-start.2 = (f32[32,512]{1,0:T(8,128)S(1)}, f32[32,512]{1,0:T(8,128)}, u32[]{:S(2)}) copy-start(f32[32,512]{1,0:T(8,128)} %refs_2_.1) | copy-start | bytes 196612
  4.6 0.8 %copy-start.3 = (bf16[96,256]{1,0:T(8,128)(2,1)S(1)}, bf16[96,256]{1,0:T(8,128)(2,1)}, u32[]{:S(2)}) copy-start(bf16[96,256]{1,0:T(8,128)(2,1)} %constant.2.clone.refs_0_) | copy-start | bytes 147460
  5.4 0.7 %copy-start.4 = (bf16[32,128]{1,0:T(8,128)(2,1)S(1)}, bf16[32,128]{1,0:T(8,128)(2,1)}, u32[]{:S(2)}) copy-start(bf16[32,128]{1,0:T(8,128)(2,1)} %refs_3_.1) | copy-start | bytes 24580

commit v2 on v1

--- a/solution.py
+++ b/solution.py
@@ -48,8 +48,9 @@
 
 
 def exchange_kernel(
-    shots, slabs, table_ref, now_ref, before_ref, velocity_ref, traces_ref, shot_ref, node_ref,
+    shots, slabs, table_hbm, now_hbm, before_hbm, velocity_hbm, traces_hbm, shot_hbm, node_hbm,
     gathered, fields, message, own, send_sem, recv_sem, field_send, field_recv,
+    table_ref, now_ref, before_ref, velocity_ref, traces_ref, shot_ref, node_ref, load_sem,
 ):
     peers = shots * slabs
     shot, slab = lax.axis_index("shot"), lax.axis_index("slab")
@@ -58,6 +59,19 @@
     groups = depth // SUB
     rows = traces_ref.shape[0]
 
+    loads = [
+        pltpu.make_async_copy(source, to, load_sem.at[i])
+        for i, (source, to) in enumerate(
+            (
+                (traces_hbm, traces_ref), (shot_hbm, shot_ref), (node_hbm, node_ref),
+                (table_hbm, table_ref), (velocity_hbm, velocity_ref),
+                (now_hbm, now_ref), (before_hbm, before_ref),
+            )
+        )
+    ]
+    for load in loads:
+        load.start()
+
     def place(d):
         index = lax.rem(me + d, peers)
         return index // slabs, lax.rem(index, slabs)
@@ -74,11 +88,8 @@
 
     lax.fori_loop(1, peers, greet, 0)
 
-    for r in range(depth):
-        to = (r % groups) * SUB + r // groups
-        own[0, to : to + 1, :] = now_ref[r : r + 1, :]
-        own[1, to : to + 1, :] = before_ref[r : r + 1, :]
-
+    for load in loads[:5]:
+        load.wait()
     parts = dot_nt(table_ref[...], traces_ref[...])
     amplitude = parts[0:ROWS] + parts[ROWS : 2 * ROWS] + parts[2 * ROWS : 3 * ROWS]
     node = node_ref[...]
@@ -125,6 +136,12 @@
 
     lax.fori_loop(0, shots, fill, 0, unroll=shots <= 8)
 
+    for load in loads[5:]:
+        load.wait()
+    for r in range(depth):
+        to = (r % groups) * SUB + r // groups
+        own[0, to : to + 1, :] = now_ref[r : r + 1, :]
+        own[1, to : to + 1, :] = before_ref[r : r + 1, :]
     pl.semaphore_wait(barrier, peers - 1)
 
     def field_copy(d):
@@ -160,17 +177,23 @@
         field_copy(d).wait()
         return carry
 
+    lax.fori_loop(1, slabs, start_field, 0)
     lax.fori_loop(1, peers, start_message, 0)
-    lax.fori_loop(1, slabs, start_field, 0)
-    gathered[slab, shot] = message[shot]
-    fields[slab] = own[...]
+    keep_message = pltpu.make_async_copy(
+        message.at[shot], gathered.at[slab, shot], load_sem.at[0]
+    )
+    keep_field = pltpu.make_async_copy(own, fields.at[slab], load_sem.at[1])
+    keep_message.start()
+    keep_field.start()
     lax.fori_loop(1, slabs, wait_field, 0)
     lax.fori_loop(1, peers, wait_message, 0)
+    keep_message.wait()
+    keep_field.wait()
 
 
 def wave_kernel(
-    shots, slabs, offset_ref, source_ref, gathered, fields, out_ref,
-    injection, left, right, courant, first, second,
+    shots, slabs, offset_ref, source_ref, gathered_hbm, fields_hbm, out_ref,
+    injection, left, right, courant, first, second, gathered, load_sem,
 ):
     depth, width = out_ref.shape
     groups = depth // SUB
@@ -178,6 +201,13 @@
     slab = lax.axis_index("slab")
     few = slabs <= 2
 
+    load_gathered = pltpu.make_async_copy(gathered_hbm, gathered, load_sem.at[0])
+    load_first = pltpu.make_async_copy(fields_hbm.at[:, 0], first, load_sem.at[1])
+    load_second = pltpu.make_async_copy(fields_hbm.at[:, 1], second, load_sem.at[2])
+    load_gathered.start()
+    load_first.start()
+    load_second.start()
+    load_gathered.wait()
     lane = lax.broadcasted_iota(jnp.int32, (SUB, LANES), 1)
     sub = lax.broadcasted_iota(jnp.int32, (SUB, LANES), 0)
     offset = offset_ref[0]
@@ -216,8 +246,6 @@
 
         lax.fori_loop(0, shots, source, 0, unroll=shots <= 8)
         injection[j] = dot_nt(left[...], right[...])
-        first[j] = fields[j, 0]
-        second[j] = fields[j, 1]
         return carry
 
     lax.fori_loop(0, slabs, prepare, 0, unroll=few)
@@ -233,6 +261,9 @@
         injection[source_slab, spot, :] = injection[source_slab, spot, :] + jnp.where(
             here, ricker_value(float(t)), 0.0
         )
+
+    load_first.wait()
+    load_second.wait()
 
     def step(t, now, other):
         def one_slab(j, carry):
@@ -312,6 +343,7 @@
     shots, slabs = lax.axis_size("shot"), lax.axis_size("slab")
     rows = traces.shape[1]
     vmem = pl.BlockSpec(memory_space=pltpu.VMEM)
+    hbm = pl.BlockSpec(memory_space=pltpu.HBM)
     smem = pl.BlockSpec(memory_space=pltpu.SMEM)
     def exchange(*refs):
         exchange_kernel(shots, slabs, *refs)
@@ -325,8 +357,8 @@
             jax.ShapeDtypeStruct((slabs, shots, 2, depth, LANES), jnp.bfloat16),
             jax.ShapeDtypeStruct((slabs, 2, depth, width), jnp.float32),
         ),
-        in_specs=[vmem] * 7,
-        out_specs=(vmem, vmem),
+        in_specs=[hbm] * 7,
+        out_specs=(hbm, hbm),
         scratch_shapes=[
             pltpu.VMEM((shots, 2, depth, LANES), jnp.bfloat16),
             pltpu.VMEM((2, depth, width), jnp.float32),
@@ -334,9 +366,17 @@
             pltpu.SemaphoreType.DMA((shots * slabs,)),
             pltpu.SemaphoreType.DMA((slabs,)),
             pltpu.SemaphoreType.DMA((slabs,)),
+            pltpu.VMEM((3 * ROWS, NS), jnp.bfloat16),
+            pltpu.VMEM((depth, width), jnp.float32),
+            pltpu.VMEM((depth, width), jnp.float32),
+            pltpu.VMEM(velocity.shape, jnp.bfloat16),
+            pltpu.VMEM((rows, NS), jnp.bfloat16),
+            pltpu.VMEM((1, rows), jnp.int32),
+            pltpu.VMEM((1, rows), jnp.int32),
+            pltpu.SemaphoreType.DMA((7,)),
         ],
         compiler_params=pltpu.CompilerParams(
-            collective_id=0, has_side_effects=True, vmem_limit_bytes=48 << 20
+            collective_id=0, has_side_effects=True, vmem_limit_bytes=63 << 20
         ),
     )(
         split_table(), field_now, field_before, velocity, traces[0],
@@ -345,7 +385,7 @@
     return pl.pallas_call(
         wave,
         out_shape=jax.ShapeDtypeStruct((depth, width), jnp.float32),
-        in_specs=[smem, smem, vmem, vmem],
+        in_specs=[smem, smem, hbm, hbm],
         out_specs=vmem,
         scratch_shapes=[
             pltpu.VMEM((slabs, STEPS * depth, width), jnp.float32),
@@ -354,8 +394,10 @@
             pltpu.VMEM((slabs, depth, width), jnp.float32),
             pltpu.VMEM((slabs, depth, width), jnp.float32),
             pltpu.VMEM((slabs, depth, width), jnp.float32),
+            pltpu.VMEM((slabs, shots, 2, depth, LANES), jnp.bfloat16),
+            pltpu.SemaphoreType.DMA((3,)),
         ],
-        compiler_params=pltpu.CompilerParams(vmem_limit_bytes=48 << 20),
+        compiler_params=pltpu.CompilerParams(vmem_limit_bytes=63 << 20),
     )(offsets, source_cell, gathered, fields)
 
 

time: 28.1 us -> 24.6 us (0.88)
  local copies, waits for them, and re-layouts: 4.76 us -> 0 us
  Pallas kernels: 21.7 us -> 23.2 us
    unnamed x14 -> x0, local copies, waits for them, and re-layouts: 4.76 us -> none
    pallas_call x1, Pallas kernels: 10.6 us -> 11.5 us  [local(): pl.pallas_call(wave, out_shape=jax.ShapeDtypeStruct((depth, width), jnp.f...]
    pallas_call x1, Pallas kernels: 11.1 us -> 11.6 us  [local(): pl.pallas_call(exchange, out_shape=(jax.ShapeDtypeStruct((slabs, shots, 2...]
where the time goes in v2:
time: 24.6 us; the launch traced here: 24.5 us
  Pallas kernels  23.2 us (94%)
  between operations  1.31 us (5%)
    pallas_call x1, Pallas kernels, local(): pl.pallas_call(exchange, out_shape=(jax.ShapeDtypeStruct((slabs, shots, 2...  11.6 us
    pallas_call x1, Pallas kernels, local(): pl.pallas_call(wave, out_shape=jax.ShapeDtypeStruct((depth, width), jnp.f...  11.5 us

profile of v2, /device:TPU:0, one launch (start us, length us, event | category | flops | bytes accessed | tf_op | source)
XLA Modules:
  0.0 24.5 jit_solution(8333098227295066177)
XLA Ops:
  1.3 11.6 %shard_map.91 = (bf16[2,8,2,32,128]{4,3,2,1,0:T(8,128)(2,1)}, f32[2,2,32,512]{3,2,1,0:T(8,128)}) custom-call(bf16[96,256]{1,0:T(8,128)(2,1)} %constant.2.clone.refs_0_, f32[32,512]{1,0:T(8,128)} %refs_1_.2, f32[32,512]{1,0:T(8,128)} %refs_2_.1, bf16[32,128]{1,0:T(8,128)(2,1)} %refs_3_.1, bf16[256,256]{1,0:T(8,128)(2,1)} %bitcast.2, s32[1,256]{1,0:T(1,128)} %bitcast.3, ...), custom_call_target="tpu_custom_call" | custom-call | tf_op jit(solution)/shard_map/pallas_call | solution.py:354
  12.9 11.5 %shard_map.92 = f32[32,512]{1,0:T(8,128)} custom-call(s32[1]{0:T(128)S(6)} %copy.10.refs_0_, s32[1]{0:T(128)S(6)} %copy.11.refs_1_, bf16[2,8,2,32,128]{4,3,2,1,0:T(8,128)(2,1)} %get-tuple-element.7.refs_2_, f32[2,2,32,512]{3,2,1,0:T(8,128)} %get-tuple-element.8.refs_3_), custom_call_target="tpu_custom_call" | custom-call | tf_op jit(solution)/shard_map/pallas_call | solution.py:385

commit v3 on v2

--- a/solution.py
+++ b/solution.py
@@ -49,12 +49,10 @@
 
 def exchange_kernel(
     shots, slabs, table_hbm, now_hbm, before_hbm, velocity_hbm, traces_hbm, shot_hbm, node_hbm,
-    gathered, fields, message, own, send_sem, recv_sem, field_send, field_recv,
+    gathered, fields, message, own, send_sem, recv_sem, field_send, field_recv, relay_send, relay_recv,
     table_ref, now_ref, before_ref, velocity_ref, traces_ref, shot_ref, node_ref, load_sem,
 ):
-    peers = shots * slabs
     shot, slab = lax.axis_index("shot"), lax.axis_index("slab")
-    me = shot * slabs + slab
     depth, width = now_ref.shape
     groups = depth // SUB
     rows = traces_ref.shape[0]
@@ -72,21 +70,24 @@
     for load in loads:
         load.start()
 
-    def place(d):
-        index = lax.rem(me + d, peers)
-        return index // slabs, lax.rem(index, slabs)
-
     barrier = pltpu.get_barrier_semaphore()
 
-    def greet(d, carry):
-        to_shot, to_slab = place(d)
+    def greet_shot(d, carry):
         pl.semaphore_signal(
-            barrier, inc=1, device_id={"shot": to_shot, "slab": to_slab},
+            barrier, inc=1, device_id={"shot": lax.rem(shot + d, shots)},
             device_id_type=pl.DeviceIdType.MESH,
         )
         return carry
 
-    lax.fori_loop(1, peers, greet, 0)
+    def greet_slab(d, carry):
+        pl.semaphore_signal(
+            barrier, inc=1, device_id={"slab": lax.rem(slab + d, slabs)},
+            device_id_type=pl.DeviceIdType.MESH,
+        )
+        return carry
+
+    lax.fori_loop(1, shots, greet_shot, 0)
+    lax.fori_loop(1, slabs, greet_slab, 0)
 
     for load in loads[:5]:
         load.wait()
@@ -124,7 +125,8 @@
         jnp.bfloat16
     )
 
-    def fill(s, carry):
+    def fill(d, carry):
+        s = lax.rem(shot + d, shots)
         mine = target == s
         to_high = jnp.where(mine, position, -1.0)
         to_low = jnp.where(mine, position + float(CAP), -1.0)
@@ -134,61 +136,91 @@
         message[s, 1] = panel
         return carry
 
-    lax.fori_loop(0, shots, fill, 0, unroll=shots <= 8)
-
+
+    def field_copy(d):
+        return pltpu.make_async_remote_copy(
+            src_ref=own, dst_ref=fields.at[slab],
+            send_sem=field_send.at[d], recv_sem=field_recv.at[d],
+            device_id={"slab": lax.rem(slab + d, slabs)},
+            device_id_type=pl.DeviceIdType.MESH,
+        )
+
+    def message_copy(d):
+        to_shot = lax.rem(shot + d, shots)
+        return pltpu.make_async_remote_copy(
+            src_ref=message.at[to_shot], dst_ref=gathered.at[slab, shot],
+            send_sem=send_sem.at[d], recv_sem=recv_sem.at[d],
+            device_id={"shot": to_shot},
+            device_id_type=pl.DeviceIdType.MESH,
+        )
+
+    def start_message(d, carry):
+        fill(d, carry)
+        message_copy(d).start()
+        return carry
+
+    def start_field(d, carry):
+        field_copy(d).start()
+        return carry
+
+    def wait_field(d, carry):
+        field_copy(d).wait()
+        return carry
+
+    def relay_copy(d, e):
+        from_shot = lax.rem(shot + shots - d, shots)
+        return pltpu.make_async_remote_copy(
+            src_ref=gathered.at[slab, from_shot], dst_ref=gathered.at[slab, from_shot],
+            send_sem=relay_send.at[e, d], recv_sem=relay_recv.at[e, d],
+            device_id={"slab": lax.rem(slab + e, slabs)},
+            device_id_type=pl.DeviceIdType.MESH,
+        )
+
+    def relay(d, carry):
+        def one(e, inner):
+            relay_copy(d, e).start()
+            return inner
+
+        return lax.fori_loop(1, slabs, one, carry)
+
+    def arrive(d, carry):
+        message_copy(d).wait_recv()
+        return relay(d, carry)
+
+    def finish(d, carry):
+        def one(e, inner):
+            relay_copy(d, e).wait()
+            return inner
+
+        return lax.fori_loop(1, slabs, one, carry)
+
+    def sent(d, carry):
+        message_copy(d).wait_send()
+        return carry
+
+    keep_message = pltpu.make_async_copy(
+        message.at[shot], gathered.at[slab, shot], load_sem.at[0]
+    )
+    keep_field = pltpu.make_async_copy(own, fields.at[slab], load_sem.at[1])
+    pl.semaphore_wait(barrier, shots - 1 + slabs - 1)
+    lax.fori_loop(1, shots, start_message, 0, unroll=shots <= 8)
+    fill(0, 0)
+    keep_message.start()
     for load in loads[5:]:
         load.wait()
     for r in range(depth):
         to = (r % groups) * SUB + r // groups
         own[0, to : to + 1, :] = now_ref[r : r + 1, :]
         own[1, to : to + 1, :] = before_ref[r : r + 1, :]
-    pl.semaphore_wait(barrier, peers - 1)
-
-    def field_copy(d):
-        return pltpu.make_async_remote_copy(
-            src_ref=own, dst_ref=fields.at[slab],
-            send_sem=field_send.at[d], recv_sem=field_recv.at[d],
-            device_id={"slab": lax.rem(slab + d, slabs)},
-            device_id_type=pl.DeviceIdType.MESH,
-        )
-
-    def message_copy(d):
-        to_shot, to_slab = place(d)
-        return pltpu.make_async_remote_copy(
-            src_ref=message.at[to_shot], dst_ref=gathered.at[slab, shot],
-            send_sem=send_sem.at[d], recv_sem=recv_sem.at[d],
-            device_id={"shot": to_shot, "slab": to_slab},
-            device_id_type=pl.DeviceIdType.MESH,
-        )
-
-    def start_message(d, carry):
-        message_copy(d).start()
-        return carry
-
-    def start_field(d, carry):
-        field_copy(d).start()
-        return carry
-
-    def wait_message(d, carry):
-        message_copy(d).wait()
-        return carry
-
-    def wait_field(d, carry):
-        field_copy(d).wait()
-        return carry
-
+    keep_field.start()
     lax.fori_loop(1, slabs, start_field, 0)
-    lax.fori_loop(1, peers, start_message, 0)
-    keep_message = pltpu.make_async_copy(
-        message.at[shot], gathered.at[slab, shot], load_sem.at[0]
-    )
-    keep_field = pltpu.make_async_copy(own, fields.at[slab], load_sem.at[1])
-    keep_message.start()
-    keep_field.start()
+    keep_message.wait()
+    relay(0, 0)
+    lax.fori_loop(1, shots, arrive, 0)
+    keep_field.wait()
     lax.fori_loop(1, slabs, wait_field, 0)
-    lax.fori_loop(1, peers, wait_message, 0)
-    keep_message.wait()
-    keep_field.wait()
+    lax.fori_loop(1, shots, sent, 0)
+    lax.fori_loop(0, shots, finish, 0)
 
 
 def wave_kernel(
@@ -362,10 +394,12 @@
         scratch_shapes=[
             pltpu.VMEM((shots, 2, depth, LANES), jnp.bfloat16),
             pltpu.VMEM((2, depth, width), jnp.float32),
-            pltpu.SemaphoreType.DMA((shots * slabs,)),
-            pltpu.SemaphoreType.DMA((shots * slabs,)),
+            pltpu.SemaphoreType.DMA((shots,)),
+            pltpu.SemaphoreType.DMA((shots,)),
             pltpu.SemaphoreType.DMA((slabs,)),
             pltpu.SemaphoreType.DMA((slabs,)),
+            pltpu.SemaphoreType.DMA((slabs, shots)),
+            pltpu.SemaphoreType.DMA((slabs, shots)),
             pltpu.VMEM((3 * ROWS, NS), jnp.bfloat16),
             pltpu.VMEM((depth, width), jnp.float32),
             pltpu.VMEM((depth, width), jnp.float32),

time: 24.6 us -> 24.4 us (level)
  no operation moved by 1% of the time
where the time goes in v3:
time: 24.4 us; the launch traced here: 24.3 us
  Pallas kernels  23 us (94%)
  between operations  1.31 us (5%)
    pallas_call x1, Pallas kernels, local(): pl.pallas_call(wave, out_shape=jax.ShapeDtypeStruct((depth, width), jnp.f...  11.5 us
    pallas_call x1, Pallas kernels, local(): pl.pallas_call(exchange, out_shape=(jax.ShapeDtypeStruct((slabs, shots, 2...  11.4 us

profile of v3, /device:TPU:0, one launch (start us, length us, event | category | flops | bytes accessed | tf_op | source)
XLA Modules:
  0.0 24.3 jit_solution(7740631786326860926)
XLA Ops:
  1.3 11.4 %shard_map.91 = (bf16[2,8,2,32,128]{4,3,2,1,0:T(8,128)(2,1)}, f32[2,2,32,512]{3,2,1,0:T(8,128)}) custom-call(bf16[96,256]{1,0:T(8,128)(2,1)} %constant.2.clone.refs_0_, f32[32,512]{1,0:T(8,128)} %refs_1_.2, f32[32,512]{1,0:T(8,128)} %refs_2_.1, bf16[32,128]{1,0:T(8,128)(2,1)} %refs_3_.1, bf16[256,256]{1,0:T(8,128)(2,1)} %bitcast.2, s32[1,256]{1,0:T(1,128)} %bitcast.3, ...), custom_call_target="tpu_custom_call" | custom-call | tf_op jit(solution)/shard_map/pallas_call | solution.py:386
  12.7 11.5 %shard_map.92 = f32[32,512]{1,0:T(8,128)} custom-call(s32[1]{0:T(128)S(6)} %copy.10.refs_0_, s32[1]{0:T(128)S(6)} %copy.11.refs_1_, bf16[2,8,2,32,128]{4,3,2,1,0:T(8,128)(2,1)} %get-tuple-element.7.refs_2_, f32[2,2,32,512]{3,2,1,0:T(8,128)} %get-tuple-element.8.refs_3_), custom_call_target="tpu_custom_call" | custom-call | tf_op jit(solution)/shard_map/pallas_call | solution.py:419

commit v4 on v3

--- a/solution.py
+++ b/solution.py
@@ -251,6 +251,7 @@
     at_cell = lax.broadcasted_iota(jnp.int32, (width, LANES), 0).astype(jnp.float32)
 
     def prepare(j, carry):
+        half = j % 2
         turned = []
         for c in range(columns + 1):
             panel = jnp.minimum(panel0 + c, shots - 1)
@@ -268,19 +269,27 @@
             values = gathered[j, s, 0].astype(jnp.float32)
             at_depth = values[STEPS : STEPS + 1]
             at_lateral = values[STEPS + 1 : STEPS + 2] * 256.0 + values[STEPS + 2 : STEPS + 3]
-            chosen = row_depth == at_depth
+            chosen = jnp.where(row_depth == at_depth, 1.0, 0.0).astype(jnp.bfloat16)
             for t in range(STEPS):
-                left[t * depth : (t + 1) * depth, lanes] = jnp.where(
-                    chosen, values[t : t + 1], 0.0
-                ).astype(jnp.bfloat16)
-            right[:, lanes] = jnp.where(at_cell == at_lateral, 1.0, 0.0).astype(jnp.bfloat16)
+                spread = jnp.broadcast_to(values[t : t + 1], (2 * SUB, LANES)).astype(
+                    jnp.bfloat16
+                )
+                for part in range(0, depth, 2 * SUB):
+                    left[half, t * depth + part : t * depth + part + 2 * SUB, lanes] = (
+                        chosen[part : part + 2 * SUB] * spread
+                    )
+            right[half, :, lanes] = jnp.where(at_cell == at_lateral, 1.0, 0.0).astype(jnp.bfloat16)
             return inner
 
         lax.fori_loop(0, shots, source, 0, unroll=shots <= 8)
-        injection[j] = dot_nt(left[...], right[...])
-        return carry
-
-    lax.fori_loop(0, slabs, prepare, 0, unroll=few)
+        injection[j] = dot_nt(left[half], right[half])
+        return carry
+
+    if few:
+        for j in range(slabs):
+            prepare(j, 0)
+    else:
+        lax.fori_loop(0, slabs, prepare, 0)
 
     source = source_ref[0]
     source_depth = source // width
@@ -362,7 +371,7 @@
         step(2 * i + 1, second, first)
         return carry
 
-    lax.fori_loop(0, STEPS // 2, pair, 0)
+    lax.fori_loop(0, STEPS // 2, pair, 0, unroll=2)
     for r in range(depth):
         at = (r % groups) * SUB + r // groups
         out_ref[r : r + 1, :] = first[slab, at : at + 1, :]
@@ -423,8 +432,8 @@
         out_specs=vmem,
         scratch_shapes=[
             pltpu.VMEM((slabs, STEPS * depth, width), jnp.float32),
-            pltpu.VMEM((STEPS * depth, shots * LANES), jnp.bfloat16),
-            pltpu.VMEM((width, shots * LANES), jnp.bfloat16),
+            pltpu.VMEM((2, STEPS * depth, shots * LANES), jnp.bfloat16),
+            pltpu.VMEM((2, width, shots * LANES), jnp.bfloat16),
             pltpu.VMEM((slabs, depth, width), jnp.float32),
             pltpu.VMEM((slabs, depth, width), jnp.float32),
             pltpu.VMEM((slabs, depth, width), jnp.float32),

time: 24.4 us -> 23.7 us (0.971)
  Pallas kernels: 23 us -> 22.2 us
    pallas_call x1, Pallas kernels: 11.5 us -> 10.8 us  [local(): pl.pallas_call(wave, out_shape=jax.ShapeDtypeStruct((depth, width), jnp.f...]
where the time goes in v4:
time: 23.7 us; the launch traced here: 23.5 us
  Pallas kernels  22.2 us (94%)
  between operations  1.31 us (6%)
    pallas_call x1, Pallas kernels, local(): pl.pallas_call(exchange, out_shape=(jax.ShapeDtypeStruct((slabs, shots, 2...  11.4 us
    pallas_call x1, Pallas kernels, local(): pl.pallas_call(wave, out_shape=jax.ShapeDtypeStruct((depth, width), jnp.f...  10.8 us

profile of v4, /device:TPU:0, one launch (start us, length us, event | category | flops | bytes accessed | tf_op | source)
XLA Modules:
  0.0 23.5 jit_solution(4497805409775627443)
XLA Ops:
  1.3 11.4 %shard_map.91 = (bf16[2,8,2,32,128]{4,3,2,1,0:T(8,128)(2,1)}, f32[2,2,32,512]{3,2,1,0:T(8,128)}) custom-call(bf16[96,256]{1,0:T(8,128)(2,1)} %constant.2.clone.refs_0_, f32[32,512]{1,0:T(8,128)} %refs_1_.2, f32[32,512]{1,0:T(8,128)} %refs_2_.1, bf16[32,128]{1,0:T(8,128)(2,1)} %refs_3_.1, bf16[256,256]{1,0:T(8,128)(2,1)} %bitcast.2, s32[1,256]{1,0:T(1,128)} %bitcast.3, ...), custom_call_target="tpu_custom_call" | custom-call | tf_op jit(solution)/shard_map/pallas_call | solution.py:395
  12.7 10.8 %shard_map.92 = f32[32,512]{1,0:T(8,128)} custom-call(s32[1]{0:T(128)S(6)} %copy.10.refs_0_, s32[1]{0:T(128)S(6)} %copy.11.refs_1_, bf16[2,8,2,32,128]{4,3,2,1,0:T(8,128)(2,1)} %get-tuple-element.7.refs_2_, f32[2,2,32,512]{3,2,1,0:T(8,128)} %get-tuple-element.8.refs_3_), custom_call_target="tpu_custom_call" | custom-call | tf_op jit(solution)/shard_map/pallas_call | solution.py:428

commit v5 on v4

--- a/solution.py
+++ b/solution.py
@@ -371,7 +371,7 @@
         step(2 * i + 1, second, first)
         return carry
 
-    lax.fori_loop(0, STEPS // 2, pair, 0, unroll=2)
+    lax.fori_loop(0, STEPS // 2, pair, 0, unroll=4)
     for r in range(depth):
         at = (r % groups) * SUB + r // groups
         out_ref[r : r + 1, :] = first[slab, at : at + 1, :]

time: 23.7 us -> 23.4 us (0.987)
  no operation moved by 1% of the time
where the time goes in v5:
time: 23.4 us; the launch traced here: 23.3 us
  Pallas kernels  22 us (94%)
  between operations  1.31 us (6%)
    pallas_call x1, Pallas kernels, local(): pl.pallas_call(exchange, out_shape=(jax.ShapeDtypeStruct((slabs, shots, 2...  11.4 us
    pallas_call x1, Pallas kernels, local(): pl.pallas_call(wave, out_shape=jax.ShapeDtypeStruct((depth, width), jnp.f...  10.5 us

profile of v5, /device:TPU:0, one launch (start us, length us, event | category | flops | bytes accessed | tf_op | source)
XLA Modules:
  0.0 23.3 jit_solution(14863572266073157564)
XLA Ops:
  1.3 11.4 %shard_map.91 = (bf16[2,8,2,32,128]{4,3,2,1,0:T(8,128)(2,1)}, f32[2,2,32,512]{3,2,1,0:T(8,128)}) custom-call(bf16[96,256]{1,0:T(8,128)(2,1)} %constant.2.clone.refs_0_, f32[32,512]{1,0:T(8,128)} %refs_1_.2, f32[32,512]{1,0:T(8,128)} %refs_2_.1, bf16[32,128]{1,0:T(8,128)(2,1)} %refs_3_.1, bf16[256,256]{1,0:T(8,128)(2,1)} %bitcast.2, s32[1,256]{1,0:T(1,128)} %bitcast.3, ...), custom_call_target="tpu_custom_call" | custom-call | tf_op jit(solution)/shard_map/pallas_call | solution.py:395
  12.7 10.5 %shard_map.92 = f32[32,512]{1,0:T(8,128)} custom-call(s32[1]{0:T(128)S(6)} %copy.10.refs_0_, s32[1]{0:T(128)S(6)} %copy.11.refs_1_, bf16[2,8,2,32,128]{4,3,2,1,0:T(8,128)(2,1)} %get-tuple-element.7.refs_2_, f32[2,2,32,512]{3,2,1,0:T(8,128)} %get-tuple-element.8.refs_3_), custom_call_target="tpu_custom_call" | custom-call | tf_op jit(solution)/shard_map/pallas_call | solution.py:428
